TPU v7x, 32 devices: a whole 2x2x4 slice. The times are simulated.
32 devices in a mesh: stream: 2 (over y), dp: 8 (over z, x), head: 2 (over core).
Axes of the slice: x: 2, y: 2, z: 4, core: 2. Of those that a mesh axis runs over, the one named last changes fastest.
Arguments:
- patches: bfloat16 [32, 512, 768], P(('dp', 'head')), may hold values from -6 to 6
- order: int32 [32, 512], P(('dp', 'head')), may hold values from 0 to 511, each once within a row
- cotangent: bfloat16 [2, 32, 256, 768], P('stream', ('dp', 'head')), may hold values from -6 to 6
- norm_gains: float32 [2, 2, 768], P('stream'), may hold values from 0.5 to 1.5
- norm_biases: float32 [2, 2, 768], P('stream'), may hold values from -3 to 3
- layer_scales: float32 [2, 2, 768], P('stream'), may hold values from 0.5 to 1.5
- qkv_weight: bfloat16 [2, 3, 768, 768], P('stream', None, None, 'head'), may hold values from -0.21875 to 0.21875
- out_weight: bfloat16 [2, 768, 768], P('stream', 'head'), may hold values from -2.5 to 2.5
- up_weight: bfloat16 [2, 768, 3072], P('stream', None, 'head'), may hold values from -0.21875 to 0.21875
- up_bias: bfloat16 [2, 3072], P('stream', 'head'), may hold values from -3 to 3
- down_weight: bfloat16 [2, 3072, 768], P('stream', 'head'), may hold values from -0.109375 to 0.109375
- down_bias: float32 [2, 768], P('stream'), may hold values from -2 to 2
- mask_token: float32 [768], replicated, may hold values from -6 to 6
Outputs:
- latents: bfloat16 [32, 256, 768], P(('dp', 'head'))
- features: bfloat16 [2, 32, 256, 768], P('stream', ('dp', 'head'))
- input_grads: float32 [2, 32, 512, 768], P('stream', ('dp', 'head'))
- norm_gains_grad: float32 [2, 2, 768], P('stream')
- norm_biases_grad: float32 [2, 2, 768], P('stream')
- layer_scales_grad: float32 [2, 2, 768], P('stream')
- qkv_grad: float32 [2, 3, 768, 768], P('stream', None, None, 'head')
- out_grad: float32 [2, 768, 768], P('stream', 'head')
- up_grad: float32 [2, 768, 3072], P('stream', None, 'head')
- up_bias_grad: float32 [2, 3072], P('stream', 'head')
- down_grad: float32 [2, 3072, 768], P('stream', 'head')
- down_bias_grad: float32 [2, 768], P('stream')
- mask_token_grad: float32 [768], replicated
Inputs may be any that keep to these rules, and one draw needn't show every extreme that they name: `order`: each row holds every patch position of its image once; the first half of a row are the visible patches, the second half the masked ones.
All inputs are finite; a program needn't handle non-finite values.
Results may differ from a plain program's by a relative error of at most 0.014.
Values may be sent and summed in bfloat16 or wider, within the bound.
A program may use at most 192 MiB of HBM per device.

v0:
```python
import functools
import math

import jax
import jax.numpy as jnp
from jax import lax
from jax.experimental import pallas as pl
from jax.experimental.pallas import tpu as pltpu
from jax.sharding import PartitionSpec as P

HEADS = 12
EPSILON = 1e-06
BF = jnp.bfloat16
F32 = jnp.float32
ROWS_AT_ONCE = 64
NN = ((1,), (0,))
NT = ((1,), (1,))
TN = ((0,), (0,))
SWAP = ((0, 1), (1, 0))
VMEM_BYTES = 60 * 1024 * 1024


def dot(left, right, dims=NN):
    return lax.dot_general(left, right, (dims, ((), ())), preferred_element_type=F32)


def row_loop(rows, body):
    def step(index, carry):
        body(pl.ds(pl.multiple_of(index * ROWS_AT_ONCE, ROWS_AT_ONCE), ROWS_AT_ONCE))
        return carry

    lax.fori_loop(0, rows // ROWS_AT_ONCE, step, 0)


def halves_loop(size, body):
    def step(half, carry):
        body(half, pl.ds(pl.multiple_of(half * size, size), size))
        return carry

    lax.fori_loop(0, 2, step, 0)


def standardize(values):
    centred = values - jnp.mean(values, -1, keepdims=True)
    inv_std = lax.rsqrt(jnp.mean(centred * centred, -1, keepdims=True) + EPSILON)
    return centred * inv_std, inv_std


def norm_into(source, target, gain, bias):
    def body(rows):
        scaled, _ = standardize(source[rows, :])
        target[rows, :] = (scaled * gain + bias).astype(BF)

    row_loop(source.shape[0], body)


def fold_rows(values):
    return jnp.sum(values.reshape(-1, 8, values.shape[-1]), 0)


def norm_back(grad, scaled, inv_std, gain):
    scaled_grad = grad * gain
    return inv_std * (
        scaled_grad
        - jnp.mean(scaled_grad, -1, keepdims=True)
        - scaled * jnp.mean(scaled_grad * scaled, -1, keepdims=True)
    )


class Weights:
    NAMES = ("qkv", "out", "up", "down")

    def __init__(self, sources, buffers, sems, names=NAMES, first_only=False):
        self.first_only = first_only
        self.buffers = dict(zip(self.NAMES, buffers))
        self.copies = {}
        for at, name in enumerate(self.NAMES):
            if name not in names:
                continue
            for half in range(2):
                self.copies[name, half] = pltpu.make_async_copy(
                    sources[2 * at + half], self.buffers[name].at[half], sems.at[at, half]
                )

    def each(self, names, method):
        def run():
            for name in names:
                for half in range(2):
                    getattr(self.copies[name, half], method)()

        if self.first_only:
            pl.when(pl.program_id(0) == 0)(run)
        else:
            run()

    def start(self, order):
        self.each(order, "start")

    def wait(self, name):
        self.each((name,), "wait")

    def __getitem__(self, name):
        return self.buffers[name]


def weight_scratch(width, local, hidden):
    return [
        pltpu.VMEM((2, 3, width, local), BF),
        pltpu.VMEM((2, local, width), BF),
        pltpu.VMEM((2, width, hidden), BF),
        pltpu.VMEM((2, hidden, width), BF),
        pltpu.SemaphoreType.DMA((4, 2)),
    ]


def head_masks():
    lanes = lax.broadcasted_iota(jnp.int32, (1, 128), 1)
    low = (lanes < 64).astype(F32)
    return low.astype(BF), (1.0 - low).astype(BF)


def forward(rows_all, ctx, vec, up_bias, weights, keep, result_fn):
    width = rows_all.shape[1]
    row_count = rows_all.shape[0] - ctx
    normed, queries, keys, values, probs, mixed = (
        keep[name] for name in ("N", "Q", "K", "V", "P", "O")
    )
    norm_into(rows_all, normed, vec[0:1, :], vec[2:3, :])
    weights.wait("qkv")
    local = weights["qkv"].shape[3]

    def project(half, cols):
        queries[:, cols] = (dot(normed[ctx:, :], weights["qkv"][half, 0]) * 0.125).astype(BF)
        keys[:, cols] = dot(normed[...], weights["qkv"][half, 1]).astype(BF)
        values[:, cols] = dot(normed[...], weights["qkv"][half, 2]).astype(BF)

    halves_loop(local, project)
    masks = head_masks()

    def attend(pair, carry):
        cols = pl.ds(pl.multiple_of(pair * 128, 128), 128)
        query, key = queries[:, cols], keys[:, cols]
        value_t = values[:, cols].T
        outs = []
        for at in range(2):
            scores = dot(key, query * masks[at], NT)
            weight = jnp.exp(scores - jnp.max(scores, 0, keepdims=True))
            prob = (weight * (1.0 / jnp.sum(weight, 0, keepdims=True))).astype(BF)
            probs[2 * pair + at] = prob
            outs.append(dot(value_t[64 * at : 64 * at + 64], prob))
        mixed[:, cols] = jnp.concatenate(outs, 0).T.astype(BF)
        return carry

    lax.fori_loop(0, HEADS // 2, attend, 0)
    weights.wait("out")
    attended = dot(mixed[:, :local], weights["out"][0]) + dot(mixed[:, local:], weights["out"][1])
    hidden, normed_two = keep["H"], keep["M"]
    keep["A"][...] = attended.astype(keep["A"].dtype)
    hidden[...] = rows_all[ctx:, :] + vec[4:5, :] * attended
    norm_into(hidden, normed_two, vec[1:2, :], vec[3:4, :])
    weights.wait("up")
    weights.wait("down")
    fed = keep["F"]
    fed[...] = jnp.broadcast_to(vec[6:7, :], fed.shape)
    step = 512
    per_half = weights["up"].shape[2] // step

    def feed(index, carry):
        half, chunk = index // per_half, index % per_half
        cols = pl.ds(pl.multiple_of(chunk * step, step), step)
        pre = dot(normed_two[...], weights["up"][half, :, cols]) + up_bias[half, :, cols]
        phi = 0.5 + 0.5 * lax.erf(pre * math.sqrt(0.5))
        act = (pre * phi).astype(BF)
        if "G" in keep:
            keep["G"][half, :, cols] = act
            density = jnp.exp(pre * pre * -0.5) * (1.0 / math.sqrt(2.0 * math.pi))
            keep["D"][half, :, cols] = (phi + pre * density).astype(BF)
        fed[...] += dot(act, weights["down"][half, cols, :])
        return carry

    lax.fori_loop(0, 2 * per_half, feed, 0)

    def finish(rows):
        result_fn(rows, hidden[rows, :] + vec[5:6, :] * fed[rows, :])

    row_loop(row_count, finish)


def backward(rows_all, ctx, out_grad_fn, vec, weights, keep, grads, work, sums, up_bias_grad):
    width = rows_all.shape[1]
    row_count = rows_all.shape[0] - ctx
    local = width // 2
    grad_in = work["dH"]
    for at in range(8):
        sums[at] = jnp.zeros((8, width), F32)

    def enter(rows):
        grad = out_grad_fn(rows)
        grad_in[rows, :] = grad
        branch = vec[5:6, :] * grad
        sums[5] += fold_rows(grad * keep["F"][rows, :].astype(F32))
        sums[6] += fold_rows(branch)
        grads["dF"][rows, :] = branch.astype(BF)

    row_loop(row_count, enter)
    weights.wait("down")
    weights.wait("up")
    grad_mid = work["dM"]
    grad_mid[...] = jnp.zeros_like(grad_mid)
    step = 512
    per_half = weights["up"].shape[2] // step

    def feed(index, carry):
        half, chunk = index // per_half, index % per_half
        cols = pl.ds(pl.multiple_of(chunk * step, step), step)
        act_grad = dot(grads["dF"][...], weights["down"][half, cols, :], NT)
        pre_grad = act_grad * keep["D"][half, :, cols].astype(F32)
        up_bias_grad[half, :, cols] = jnp.sum(pre_grad, 0, keepdims=True)
        pre_grad = pre_grad.astype(BF)
        grads["dU"][half, :, cols] = pre_grad
        grad_mid[...] += dot(pre_grad, weights["up"][half, :, cols], NT)
        return carry

    lax.fori_loop(0, 2 * per_half, feed, 0)

    def middle(rows):
        scaled, inv_std = standardize(keep["H"][rows, :])
        grad = grad_mid[rows, :]
        sums[1] += fold_rows(grad * scaled)
        sums[3] += fold_rows(grad)
        hidden_grad = grad_in[rows, :] + norm_back(grad, scaled, inv_std, vec[1:2, :])
        grad_in[rows, :] = hidden_grad
        sums[4] += fold_rows(hidden_grad * keep["A"][rows, :].astype(F32))
        grads["dA"][rows, :] = (vec[4:5, :] * hidden_grad).astype(BF)

    row_loop(row_count, middle)
    weights.wait("out")
    mix_grad = work["dO"]

    def unmix(half, cols):
        mix_grad[:, cols] = dot(grads["dA"][...], weights["out"][half], NT).astype(BF)

    halves_loop(local, unmix)
    masks = head_masks()

    def attend(pair, carry):
        cols = pl.ds(pl.multiple_of(pair * 128, 128), 128)
        query, key, value = keep["Q"][:, cols], keep["K"][:, cols], keep["V"][:, cols]
        out_grad = mix_grad[:, cols]
        key_t = key.T
        value_grad = key_grad = None
        query_grads = []
        for at in range(2):
            prob = keep["P"][2 * pair + at]
            own_grad = out_grad * masks[at]
            part = dot(prob, own_grad)
            value_grad = part if value_grad is None else value_grad + part
            prob_grad = dot(value, own_grad, NT)
            wide = prob.astype(F32)
            product = wide * prob_grad
            score_grad = (product - wide * jnp.sum(product, 0, keepdims=True)).astype(BF)
            part = dot(score_grad, query * masks[at])
            key_grad = part if key_grad is None else key_grad + part
            query_grads.append(dot(key_t[64 * at : 64 * at + 64], score_grad))
        grads["dV"][:, cols] = value_grad.astype(BF)
        grads["dK"][:, cols] = key_grad.astype(BF)
        grads["dQ"][:, cols] = (jnp.concatenate(query_grads, 0).T * 0.125).astype(BF)
        return carry

    lax.fori_loop(0, HEADS // 2, attend, 0)
    weights.wait("qkv")
    grad_all = work["dN"]
    qkv = weights["qkv"]
    grad_all[...] = jnp.zeros_like(grad_all)

    def unproject(half, cols):
        grad_all[...] += dot(grads["dK"][:, cols], qkv[half, 1], NT) + dot(
            grads["dV"][:, cols], qkv[half, 2], NT
        )
        grad_all[ctx:, :] += dot(grads["dQ"][:, cols], qkv[half, 0], NT)

    halves_loop(local, unproject)

    def leave(rows):
        scaled, inv_std = standardize(rows_all[rows, :])
        grad = grad_all[rows, :]
        sums[0] += fold_rows(grad * scaled)
        sums[2] += fold_rows(grad)
        grad_all[rows, :] = norm_back(grad, scaled, inv_std, vec[0:1, :])

    row_loop(rows_all.shape[0], leave)


def write_sums(sums, target):
    for at in range(8):
        target[at : at + 1, :] = jnp.sum(sums[at], 0, keepdims=True)


def pick_rows(order_column, patches):
    places = lax.broadcasted_iota(jnp.int32, (order_column.shape[0], patches.shape[0]), 1)
    return dot((places == order_column).astype(F32).astype(BF), patches)


KEPT = ("X", "N", "Q", "K", "V", "P", "O", "A", "H", "M", "G", "D", "F")
GRADS = ("dF", "dU", "dA", "dQ", "dK", "dV")
OPERANDS = ("dF", "G", "dU", "M", "dA", "O", "dQ", "dK", "dV", "N")


def kept_shapes(rows, keys, width, hidden):
    return {
        "X": ((rows, width), BF),
        "N": ((keys, width), BF),
        "Q": ((rows, width), BF),
        "K": ((keys, width), BF),
        "V": ((keys, width), BF),
        "P": ((HEADS, keys, rows), BF),
        "O": ((rows, width), BF),
        "A": ((rows, width), BF),
        "H": ((rows, width), F32),
        "M": ((rows, width), BF),
        "G": ((2, rows, hidden), BF),
        "D": ((2, rows, hidden), BF),
        "F": ((rows, width), F32),
    }


def grad_shapes(rows, keys, width, hidden):
    return {
        "dF": ((rows, width), BF),
        "dU": ((2, rows, hidden), BF),
        "dA": ((rows, width), BF),
        "dQ": ((rows, width), BF),
        "dK": ((keys, width), BF),
        "dV": ((keys, width), BF),
    }


def vmem(shape_type):
    return pltpu.VMEM(*shape_type)


ONCE = pl.Buffered(1)


def whole(shape):
    return pl.BlockSpec(tuple(shape), lambda _: (0,) * len(shape), pipeline_mode=ONCE)


def image_of(array, image):
    return pl.BlockSpec(
        (None,) + array.shape[1:],
        lambda _: (image,) + (0,) * (array.ndim - 1),
        pipeline_mode=ONCE,
    )


ANY = pl.BlockSpec(memory_space=pl.ANY)


def shape_of(shape_type):
    return jax.ShapeDtypeStruct(*shape_type)


def nothing(shapes):
    return pl.pallas_call(
        lambda *refs: None,
        out_shape=[shape_of(s) for s in shapes],
        out_specs=[ANY] * len(shapes),
        name="no_values",
    )()


def params_of(**extra):
    return pltpu.CompilerParams(vmem_limit_bytes=VMEM_BYTES, **extra)


def block_cost(rows, keys, width, hidden, passes):
    flops = 2 * rows * width * (2 * width + 4 * hidden) + 4 * keys * width * width
    flops += 4 * rows * keys * width
    return pl.CostEstimate(flops=passes * flops, bytes_accessed=24_000_000, transcendentals=0)


def encoder_forward(image, which, patches, order_column, vec, up_bias, matrices, save):
    images, places, width = patches.shape
    rows = places // 2
    hidden = matrices[4].shape[1]
    local = width // 2
    shapes = kept_shapes(rows, rows, width, hidden)
    names = [n for n in KEPT]

    def kernel(patch_ref, order_ref, vec_ref, bias_ref, *refs):
        sources, refs = refs[:8], refs[8:]
        result, refs = refs[0], refs[1:]
        if save:
            keep = dict(zip(names, refs[: len(names)]))
            refs = refs[len(names) :]
        else:
            own = [n for n in names if n not in ("X", "G", "D")]
            keep = dict(zip(own, refs[: len(own)]))
            refs = refs[len(own) :]
        rows_ref, refs = refs[0], refs[1:]
        weights = Weights(sources, refs[:4], refs[4], first_only=not save)
        weights.start(("qkv", "out", "up", "down"))
        rows_ref[...] = pick_rows(order_ref[...], patch_ref[...])
        if save:
            keep["X"][...] = rows_ref[...].astype(BF)

        def result_fn(rows_at, value):
            result[rows_at, :] = value.astype(BF)

        forward(rows_ref, 0, vec_ref, bias_ref, weights, keep, result_fn)

    out_shapes = [((rows, width), BF)] + ([shapes[n] for n in names] if save else [])
    out_specs = [whole(s[0]) for s in out_shapes]
    patch_spec = image_of(patches, image)
    scratch = [] if save else [vmem(shapes[n]) for n in names if n not in ("X", "G", "D")]
    scratch = scratch + [pltpu.VMEM((rows, width), F32)] + weight_scratch(width, local, hidden)
    order_spec = pl.BlockSpec(
        (None, rows, 1), lambda _: (image, which, 0), pipeline_mode=ONCE
    )
    if not save:
        out_shapes = [((images, rows, width), BF)]
        out_specs = [pl.BlockSpec((None, rows, width), lambda i: (i, 0, 0))]
        patch_spec = pl.BlockSpec((None, places, width), lambda i: (i, 0, 0))
        order_spec = pl.BlockSpec((None, rows, 1), lambda i: (i, which, 0))
    return pl.pallas_call(
        kernel,
        grid=(1 if save else images,),
        out_shape=[shape_of(s) for s in out_shapes],
        in_specs=[patch_spec, order_spec, whole(vec.shape), whole(up_bias.shape)] + [ANY] * 8,
        out_specs=out_specs,
        scratch_shapes=scratch,
        compiler_params=params_of(),
        cost_estimate=block_cost(rows, rows, width, hidden, 1),
        name="encoder_forward" if save else "encoder_targets",
    )(patches, order_column, vec, up_bias, *matrices)


def encoder_backward(image, latent_grad, cotangent, order_row, kept, vec, matrices):
    rows, width = latent_grad.shape
    hidden = matrices[4].shape[1]
    local = width // 2
    shapes = grad_shapes(rows, rows, width, hidden)
    names = list(GRADS)

    def kernel(back_ref, cot_ref, order_ref, vec_ref, *refs):
        sources, refs = refs[:8], refs[8:]
        keep = dict(zip(KEPT, refs[: len(KEPT)]))
        refs = refs[len(KEPT) :]
        input_grad, vec_grad, bias_grad, refs = refs[0], refs[1], refs[2], refs[3:]
        grads = dict(zip(names, refs[: len(names)]))
        refs = refs[len(names) :]
        rows_ref, d_hidden, d_mid, d_out, d_norm, sums = refs[:6]
        weights = Weights(sources, refs[6:10], refs[10])
        weights.start(("down", "up", "out", "qkv"))
        work = {"dH": d_hidden, "dM": d_mid, "dO": d_out, "dN": d_norm}
        rows_ref[...] = keep["X"][...].astype(F32)

        def out_grad_fn(rows_at):
            return cot_ref[rows_at, :].astype(F32) + back_ref[rows_at, :].astype(F32)

        backward(rows_ref, 0, out_grad_fn, vec_ref, weights, keep, grads, work, sums, bias_grad)
        write_sums(sums, vec_grad)

        def join(rows_at):
            total = d_norm[rows_at, :] + d_hidden[rows_at, :]
            high = total.astype(BF)
            d_out[rows_at, :] = high
            grads_low[rows_at, :] = (total - high.astype(F32)).astype(BF)

        grads_low = refs[11]
        row_loop(rows, join)

        def place(index, carry):
            first = pl.multiple_of(index * 128, 128)
            places = lax.broadcasted_iota(jnp.int32, (128, rows), 0) + first
            hot = (places == order_ref[...]).astype(F32).astype(BF)
            input_grad[pl.ds(first, 128), :] = dot(hot, d_out[...]) + dot(hot, grads_low[...])
            return carry

        lax.fori_loop(0, input_grad.shape[0] // 128, place, 0)

    out_shapes = [((2 * rows, width), F32), ((8, width), F32), ((2, 1, hidden), F32)]
    out_shapes += [shapes[n] for n in names]
    scratch = [
        pltpu.VMEM((rows, width), F32),
        pltpu.VMEM((rows, width), F32),
        pltpu.VMEM((rows, width), F32),
        pltpu.VMEM((rows, width), BF),
        pltpu.VMEM((rows, width), F32),
        pltpu.VMEM((8, 8, width), F32),
    ]
    scratch += weight_scratch(width, local, hidden) + [pltpu.VMEM((rows, width), BF)]
    order_spec = pl.BlockSpec((None, 1, rows), lambda _: (image, 0, 0), pipeline_mode=ONCE)
    outs = pl.pallas_call(
        kernel,
        grid=(1,),
        out_shape=[shape_of(s) for s in out_shapes],
        in_specs=[whole(latent_grad.shape), image_of(cotangent, image), order_spec, whole(vec.shape)]
        + [ANY] * 8
        + [whole(k.shape) for k in kept],
        out_specs=[whole(s[0]) for s in out_shapes],
        scratch_shapes=scratch,
        compiler_params=params_of(),
        cost_estimate=block_cost(rows, rows, width, hidden, 1),
        name="encoder_backward",
    )(latent_grad, cotangent, order_row, vec, *matrices, *kept)
    return tuple(outs)


def operand_shapes(rows, keys, width, hidden):
    shapes = dict(grad_shapes(rows, keys, width, hidden))
    shapes.update(kept_shapes(rows, keys, width, hidden))
    return [shapes[n] for n in OPERANDS]


def regressor_block(image, latent, codes, token, cotangent, vec, up_bias, matrices):
    ctx, width = latent.shape
    rows = codes.shape[1] - ctx
    keys = rows + ctx
    hidden = matrices[4].shape[1]
    local = width // 2
    kept = kept_shapes(rows, keys, width, hidden)
    shapes = grad_shapes(rows, keys, width, hidden)
    own = [n for n in KEPT if n != "X" and n not in OPERANDS]

    def kernel(latent_ref, code_ref, token_ref, cot_ref, vec_ref, bias_ref, *refs):
        sources, refs = refs[:8], refs[8:]
        result, back, input_grad, vec_grad, bias_grad = refs[:5]
        refs = refs[5:]
        named = dict(zip(OPERANDS, refs[: len(OPERANDS)]))
        refs = refs[len(OPERANDS) :]
        keep = dict(named)
        keep.update(zip(own, refs[: len(own)]))
        refs = refs[len(own) :]
        rows_ref, d_hidden, d_mid, d_out, sums = refs[:5]
        weights = Weights(sources, refs[5:9], refs[9])
        weights.start(("qkv", "out", "up", "down"))

        def fill(rows_at):
            rows_ref[rows_at, :] = latent_ref[rows_at, :].astype(F32) + code_ref[rows_at, :]
            lower = pl.ds(rows_at.start + ctx, ROWS_AT_ONCE)
            rows_ref[lower, :] = token_ref[...] + code_ref[lower, :]

        row_loop(ctx, fill)

        def result_fn(rows_at, value):
            result[rows_at, :] = value.astype(BF)

        forward(rows_ref, ctx, vec_ref, bias_ref, weights, keep, result_fn)
        work = {"dH": d_hidden, "dM": d_mid, "dO": d_out, "dN": input_grad}

        def out_grad_fn(rows_at):
            return cot_ref[rows_at, :].astype(F32)

        weights.wait = lambda name: None
        backward(
            rows_ref, ctx, out_grad_fn, vec_ref, weights, keep, named, work, sums, bias_grad
        )

        def leave(rows_at):
            back[rows_at, :] = input_grad[rows_at, :].astype(BF)
            lower = pl.ds(rows_at.start + ctx, ROWS_AT_ONCE)
            total = input_grad[lower, :] + d_hidden[rows_at, :]
            input_grad[lower, :] = total
            sums[7] += fold_rows(total)

        row_loop(rows, leave)
        write_sums(sums, vec_grad)

    out_shapes = [
        ((rows, width), BF),
        ((ctx, width), BF),
        ((keys, width), F32),
        ((8, width), F32),
        ((2, 1, hidden), F32),
    ] + operand_shapes(rows, keys, width, hidden)
    scratch = [vmem(kept[n]) for n in own]
    scratch += [
        pltpu.VMEM((keys, width), F32),
        pltpu.VMEM((rows, width), F32),
        pltpu.VMEM((rows, width), F32),
        pltpu.VMEM((rows, width), BF),
        pltpu.VMEM((8, 8, width), F32),
    ]
    scratch += weight_scratch(width, local, hidden)
    outs = pl.pallas_call(
        kernel,
        grid=(1,),
        out_shape=[shape_of(s) for s in out_shapes],
        in_specs=[
            whole(latent.shape),
            image_of(codes, image),
            whole(token.shape),
            image_of(cotangent, image),
            whole(vec.shape),
            whole(up_bias.shape),
        ]
        + [ANY] * 8,
        out_specs=[whole(s[0]) for s in out_shapes],
        scratch_shapes=scratch,
        compiler_params=params_of(),
        cost_estimate=block_cost(rows, keys, width, hidden, 2),
        name="regressor_block",
    )(latent, codes, token, cotangent, vec, up_bias, *matrices)
    return outs


def weight_grad(name, lefts, rights, first_rows, split_left, step, halves):
    images = len(lefts)
    wide = (lefts if split_left else rights)[0]
    other = (rights if split_left else lefts)[0]
    if wide.ndim == 3:
        blocks = (wide.shape[0], wide.shape[2] // step)
        wide_spec = pl.BlockSpec((None, wide.shape[1], step), lambda h, c: (h, 0, c))
        width = wide.shape[2]
    else:
        blocks = (halves, wide.shape[1] // halves // step)
        wide_spec = pl.BlockSpec(
            (wide.shape[0], step), lambda h, c: (0, h * blocks[1] + c)
        )
        width = wide.shape[1] // halves
    other_spec = pl.BlockSpec(other.shape, lambda h, c: (0, 0))
    if split_left:
        out = ((halves, width, other.shape[1]), BF)
        out_spec = pl.BlockSpec((None, step, other.shape[1]), lambda h, c: (h, c, 0))
    else:
        out = ((halves, other.shape[1], width), BF)
        out_spec = pl.BlockSpec((None, other.shape[1], step), lambda h, c: (h, 0, c))

    def kernel(*refs):
        total = None
        for at in range(images):
            left, right = refs[at][...], refs[images + at][...]
            if first_rows:
                left = left[first_rows:]
            part = dot(left, right, TN)
            total = part if total is None else total + part
        refs[-1][...] = total.astype(BF)

    specs = ([wide_spec] * images + [other_spec] * images) if split_left else (
        [other_spec] * images + [wide_spec] * images
    )
    rows = rights[0].shape[-2]
    return pl.pallas_call(
        kernel,
        grid=blocks,
        out_shape=shape_of(out),
        in_specs=specs,
        out_specs=out_spec,
        compiler_params=params_of(),
        cost_estimate=pl.CostEstimate(
            flops=2 * images * rows * halves * width * other.shape[1],
            bytes_accessed=8_000_000,
            transcendentals=0,
        ),
        name=name,
    )(*lefts, *rights)


def matrix_grads(operands, ctx):
    named = [dict(zip(OPERANDS, one)) for one in operands]

    def column(name):
        return [one[name] for one in named]

    down = weight_grad("down_grad", column("G"), column("dF"), 0, True, 512, 2)
    up = weight_grad("up_grad", column("M"), column("dU"), 0, False, 512, 2)
    out = weight_grad("out_grad", column("O"), column("dA"), 0, True, 384, 2)
    query = weight_grad("query_grad", column("N"), column("dQ"), ctx, False, 384, 2)
    key = weight_grad("key_grad", column("N"), column("dK"), 0, False, 384, 2)
    value = weight_grad("value_grad", column("N"), column("dV"), 0, False, 384, 2)
    return down, up, out, query, key, value


UNIT = 128
LAG = 2
GIVE = 8


class Exchange:
    LINE = 4
    WIDE = 10
    DEEP = 8
    UNITS = 2 * WIDE + 2 * DEEP


def exchange_kernel(images, *refs):
    count = len(OPERANDS)
    sources = []
    for _ in range(2):
        sources.append([dict(zip(OPERANDS, refs[at * count :])) for at in range(images)])
        refs = refs[images * count :]
    vec_refs, bias_refs, refs = refs[:images], refs[images : 2 * images], refs[2 * images :]
    down_ref, up_ref, out_ref, qkv_ref = (ref.at[0] for ref in refs[:4])
    totals_ref, other_ref = refs[4:6]
    refs = refs[6:]
    held = dict(zip(OPERANDS, refs[:count]))
    acc, gives, wide_out = refs[count : count + 3]
    refs = refs[count + 3 :]
    total, own_half, from_column, from_line, from_deep, from_side, done = refs[:7]
    small_ref, small_own, small_half, small_side, small_line = refs[7:12]
    (load_sem, half_send, half_recv, x1_send, x1_recv, x2_send, x2_recv, z1_send, z1_recv) = refs[12:21]
    (z2_send, z2_recv, ax_send, ax_recv, a2_send, a2_recv, a1_send, a1_recv) = refs[21:29]
    (a4_send, a4_recv, out_sem, s_send, s_recv) = refs[29:34]
    line, wide, deep = Exchange.LINE, Exchange.WIDE, Exchange.DEEP
    dp = lax.axis_index("dp")
    place, column = dp // 2, dp % 2
    side = {"dp": place * 2 + 1 - column}
    partner = {"head": 1 - lax.axis_index("head")}
    mirror = {"stream": 1 - lax.axis_index("stream")}

    def along(direction, ahead):
        return {"dp": dp + 2 * (2 * direction - 1) * ahead}

    ranks = (line - 1 - place, place)

    stream = lax.axis_index("stream")
    rows, width = held["M"].shape[1:]
    hidden = held["G"].shape[3]
    local = width // 2

    def load(names, method):
        for which in range(2):

            @pl.when(stream == which)
            def _():
                for image, source in enumerate(sources[which]):
                    for name in names:
                        at = OPERANDS.index(name)
                        target = held[name].at[image]
                        if source[name].shape != target.shape:
                            target = target.at[pl.ds(0, source[name].shape[0]), :]
                        copy = pltpu.make_async_copy(source[name], target, load_sem.at[at, image])
                        getattr(copy, method)()

    soon = ("G", "dF", "M", "dU")
    rest = tuple(name for name in OPERANDS if name not in soon)
    load(soon, "start")
    load(rest, "start")

    def unit(buffer, at):
        return buffer.at[pl.ds(pl.multiple_of(at * UNIT, UNIT), UNIT), :]

    def remote(source, target, send, recv, device):
        return pltpu.make_async_remote_copy(
            src_ref=source,
            dst_ref=target,
            send_sem=send,
            recv_sem=recv,
            device_id=device,
            device_id_type=pl.DeviceIdType.MESH,
        )

    barrier = pltpu.get_barrier_semaphore()

    def greet(device):
        pl.semaphore_signal(barrier, inc=1, device_id=device, device_id_type=pl.DeviceIdType.MESH)

    for device in (partner, side, mirror):
        greet(device)
    for ahead in range(1, line):
        greet({"dp": ((place + ahead) % line) * 2 + column})
    pl.semaphore_wait(barrier, 2 + line)

    small_ref[...] = jnp.zeros_like(small_ref)
    small_ref[0:8, :] = sum(ref[...] for ref in vec_refs)
    for half in range(2):
        for at in range(hidden // width):
            row = 8 * (half + 1) + at
            cols = slice(at * width, (at + 1) * width)
            small_ref[row : row + 1, :] = sum(ref[half, :, cols] for ref in bias_refs)
    small_out = remote(small_ref, small_half, s_send.at[1], s_recv.at[0], partner)
    small_out.start()

    first_up = hidden // UNIT
    first_out = 2 * first_up
    first_pair = first_out + local // UNIT
    first_query = first_pair + width // UNIT
    bounds = (0, first_up, first_out, first_pair, first_query, Exchange.UNITS)

    def by_kind(at, bodies):
        for kind, one in enumerate(bodies):

            @pl.when((at >= bounds[kind]) & (at < bounds[kind + 1]))
            def _():
                one(at - bounds[kind])

    def block(at, size=UNIT):
        return pl.ds(pl.multiple_of(at * size, size), size)

    def summed(one):
        parts = [one(image) for image in range(images)]
        return functools.reduce(jnp.add, parts)

    def product(at, half):
        cols = slice(half * local, (half + 1) * local)
        query_rows = pl.ds(pl.multiple_of(stream * rows, rows), rows)

        def down(index):
            acc[...] = summed(
                lambda i: dot(held["G"][i, half, :, block(index)], held["dF"][i], TN)
            )

        def up(index):
            per = width // UNIT
            acc[...] = summed(
                lambda i: dot(
                    held["M"][i, :, block(index % per)],
                    held["dU"][i, half, :, block(index // per, width)],
                    TN,
                )
            )

        def out(index):
            acc[...] = summed(
                lambda i: dot(
                    held["O"][i, :, block(half * (local // UNIT) + index)], held["dA"][i], TN
                )
            )

        def pair(index):
            def part(name, keys):
                return summed(
                    lambda i: dot(held["N"][i, keys, block(index)], held[name][i, keys, cols], TN)
                )

            acc[:, :local] = part("dK", slice(0, rows))
            acc[:, local:] = part("dV", slice(0, rows))

            @pl.when(stream == 1)
            def _():
                acc[:, :local] += part("dK", slice(rows, None))
                acc[:, local:] += part("dV", slice(rows, None))

        def query(index):
            for at in range(2):
                acc[:, at * local : (at + 1) * local] = summed(
                    lambda i: dot(
                        held["N"][i, query_rows, block(at * (local // UNIT) + index)],
                        held["dQ"][i, :, cols],
                        TN,
                    )
                )

        by_kind(at, (down, up, out, pair, query))

    def chunks(body):
        def step(index, carry):
            body(pl.multiple_of(index * 32, 32))
            return carry

        lax.fori_loop(0, UNIT // 32, step, 0)

    def half_copy(slot, at):
        return remote(
            unit(gives, slot), unit(own_half, at), half_send.at[slot], half_recv.at[at], partner
        )

    def unit_of(step, index):
        second = index * (3 - index) // 2
        own = index // 2
        wide_unit = 2 * step + 1 - column + own * (2 * column - 1)
        return wide_unit + second * (2 * wide + 2 * step + own - wide_unit), second

    def make_give(step):
        def body(index, carry):
            at, second = unit_of(step, index)

            @pl.when((step < wide) & (second * step < deep))
            def _():
                slot = (4 * step + index) % GIVE

                @pl.when(4 * step >= GIVE)
                def _():
                    half_copy(slot, at).wait_send()

                product(at, 1)

                def convert(offset):
                    gives[pl.ds(pl.multiple_of(slot * UNIT + offset, 32), 32), :] = acc[
                        pl.ds(offset, 32), :
                    ].astype(BF)

                chunks(convert)
                half_copy(slot, at).start()

            return carry

        lax.fori_loop(0, 4, body, 0)

    def make_own(step):
        def body(index, carry):
            at, second = unit_of(step, index)

            @pl.when((step >= 0) & (step < wide) & (second * step < deep))
            def _():
                product(at, 0)
                half_copy(0, at).wait_recv()

                def join(offset):
                    where = pl.ds(pl.multiple_of(at * UNIT + offset, 32), 32)
                    total[where, :] = (
                        acc[pl.ds(offset, 32), :] + own_half[where, :].astype(F32)
                    ).astype(BF)

                chunks(join)

                @pl.when(index == 0)
                def _():
                    x1(step).start()

                for direction in range(2):

                    @pl.when((index == 1 + direction) & (ranks[direction] == 0))
                    def _():
                        z1(direction, step).start()

            return carry

        lax.fori_loop(0, 4, body, 0)

    def add(target, at, first, first_at, second, second_at):
        def body(index, carry):
            offset = index * 32
            left = first[pl.ds(pl.multiple_of(first_at * UNIT + offset, 32), 32), :]
            right = second[pl.ds(pl.multiple_of(second_at * UNIT + offset, 32), 32), :]
            target[pl.ds(pl.multiple_of(at * UNIT + offset, 32), 32), :] = (
                left.astype(F32) + right.astype(F32)
            ).astype(BF)
            return carry

        lax.fori_loop(0, UNIT // 32, body, 0)

    def x1(at):
        return remote(
            unit(total, 2 * at + 1 - column), unit(from_column, at), x1_send.at[at], x1_recv.at[at], side
        )

    def x2(direction, at, ahead=1):
        slot = direction * (wide // 2) + at
        return remote(
            unit(total, 4 * at + 2 * direction + column),
            unit(from_line, slot),
            x2_send.at[slot],
            x2_recv.at[slot],
            along(direction, ahead),
        )

    def z1(direction, at):
        slot = direction * deep + at
        return remote(
            unit(total, 2 * wide + 2 * at + direction),
            unit(from_deep, slot),
            z1_send.at[slot],
            z1_recv.at[slot],
            along(direction, 1),
        )

    def z2(direction, at):
        return remote(
            unit(total, 2 * wide + 2 * at + direction),
            unit(from_side, at // 2),
            z2_send.at[at // 2],
            z2_recv.at[at // 2],
            side,
        )

    def finished(at, send, recv, slot, device):
        return remote(unit(done, at), unit(done, at), send.at[slot], recv.at[slot], device)

    def ax(at, sent):
        parity = column if sent else 1 - column
        return finished(2 * at + parity, ax_send, ax_recv, at, side)

    def a2(direction, at):
        slot = direction * (wide // 2) + at
        return finished(
            4 * at + 2 * direction + column, a2_send, a2_recv, slot, along(direction, -1)
        )

    def a1(direction, at):
        slot = direction * deep + at
        return finished(
            2 * wide + 2 * at + direction, a1_send, a1_recv, slot, along(direction, -1)
        )

    def a4(direction, at):
        return finished(2 * wide + 2 * at + direction, a4_send, a4_recv, at // 2, side)

    def put(at):
        def widen(offset):
            where = pl.ds(pl.multiple_of(at * UNIT + offset, 32), 32)
            wide_out[where, :] = done[where, :].astype(F32)

        chunks(widen)

        def send(target, cols=slice(None)):
            pltpu.make_async_copy(unit(wide_out, at).at[:, cols], target, out_sem.at[at]).start()

        left, right = pl.ds(0, local), pl.ds(local, local)

        def up(index):
            per = width // UNIT
            send(up_ref.at[block(index % per), block(index // per, width)])

        def pair(index):
            send(qkv_ref.at[1, block(index), :], left)
            send(qkv_ref.at[2, block(index), :], right)

        def query(index):
            send(qkv_ref.at[0, block(index), :], left)
            send(qkv_ref.at[0, block(local // UNIT + index), :], right)

        by_kind(
            at,
            (
                lambda index: send(down_ref.at[block(index), :]),
                up,
                lambda index: send(out_ref.at[block(index), :]),
                pair,
                query,
            ),
        )

    def small_phase(step):
        @pl.when(step == 2)
        def _():
            small_out.wait_recv()
            small_own[0:8, :] = small_ref[0:8, :] + small_half[0:8, :]
            small_own[8:16, :] = small_ref[8:16, :] + small_half[16:24, :]
            small_side_copy().start()

        @pl.when(step == 4)
        def _():
            small_side_copy().wait_recv()
            small_line[place] = small_own[...] + small_side[...]
            for ahead in range(1, line):
                small_line_copy(ahead).start()

        @pl.when(step == 8)
        def _():
            for ahead in range(1, line):
                small_line_copy(ahead).wait_recv()
            summed = small_line[0]
            for at in range(1, line):
                summed = summed + small_line[at]
            totals_ref[...] = summed
            small_mirror_copy().start()

    def small_side_copy():
        return remote(small_own, small_side, s_send.at[2], s_recv.at[1], side)

    def small_line_copy(ahead):
        there = (place + ahead) % line
        return remote(
            small_line.at[place],
            small_line.at[place],
            s_send.at[2 + ahead],
            s_recv.at[1 + ahead],
            {"dp": there * 2 + column},
        )

    def small_mirror_copy():
        return remote(
            totals_ref, other_ref, s_send.at[2 + line], s_recv.at[1 + line], mirror
        )

    def step_body(step, carry):
        @pl.when(step == 1)
        def _():
            load(rest, "wait")

        make_give(step + 1)
        make_own(step)

        at = step - LAG

        @pl.when((at >= 0) & (at < wide))
        def _():
            x1(at).wait_recv()
            add(total, 2 * at + column, total, 2 * at + column, from_column, at)
            for direction in range(2):

                @pl.when((at % 2 == direction) & (ranks[direction] == 0))
                def _():
                    x2(direction, at // 2).start()

        for direction in range(2):
            rank = ranks[direction]
            at = step - LAG * rank

            @pl.when((rank >= 1) & (at >= 0) & (at < deep))
            def _():
                where = 2 * wide + 2 * at + direction
                z1(direction, at).wait_recv()
                add(total, where, total, where, from_deep, direction * deep + at)

                @pl.when(rank < line - 1)
                def _():
                    z1(direction, at).start()

                @pl.when((rank == line - 1) & (at % 2 != column))
                def _():
                    z2(direction, at).start()

            twice = step - LAG - LAG * rank - direction

            @pl.when((rank >= 1) & (twice >= 0) & (twice < wide) & (twice % 2 == 0))
            def _():
                at = twice // 2
                where = 4 * at + 2 * direction + column
                x2(direction, at).wait_recv()
                slot = direction * (wide // 2) + at

                @pl.when(rank < line - 1)
                def _():
                    add(total, where, total, where, from_line, slot)
                    x2(direction, at).start()

                @pl.when(rank == line - 1)
                def _():
                    add(done, where, total, where, from_line, slot)
                    a2(direction, at).start()
                    ax(2 * at + direction, True).start()
                    put(where)

            at = step - LAG * line

            @pl.when((rank == line - 1) & (at >= 0) & (at < deep) & (at % 2 == column))
            def _():
                where = 2 * wide + 2 * at + direction
                z2(direction, at).wait_recv()
                add(done, where, total, where, from_side, at // 2)
                a1(direction, at).start()
                a4(direction, at).start()
                put(where)

            later = step - LAG * line - LAG

            @pl.when((rank == line - 1) & (later >= 0) & (later < deep) & (later % 2 != column))
            def _():
                a4(direction, later).wait_recv()
                a1(direction, later).start()
                put(2 * wide + 2 * later + direction)

            back = LAG * (line - 1 - rank)
            twice = step - LAG * line - back - direction

            @pl.when((rank < line - 1) & (twice >= 0) & (twice < wide) & (twice % 2 == 0))
            def _():
                at = twice // 2
                a2(direction, at).wait_recv()

                @pl.when(rank > 0)
                def _():
                    a2(direction, at).start()

                ax(2 * at + direction, True).start()
                put(4 * at + 2 * direction + column)

            for other in range(2):
                at = step - LAG * line - back - LAG * other

                @pl.when(
                    (rank < line - 1)
                    & (at >= 0)
                    & (at < deep)
                    & ((at + column) % 2 == other)
                )
                def _():
                    a1(direction, at).wait_recv()

                    @pl.when(rank > 0)
                    def _():
                        a1(direction, at).start()

                    put(2 * wide + 2 * at + direction)

            twice = step - LAG * line - back - direction - LAG

            @pl.when((twice >= 0) & (twice < wide) & (twice % 2 == 0))
            def _():
                at = twice + direction
                ax(at, False).wait_recv()
                put(2 * at + 1 - column)

        small_phase(step)
        return carry

    steps = wide - 1 + LAG * line + LAG * (line - 1) + LAG + 1
    load(soon, "wait")
    lax.fori_loop(-1, steps, step_body, 0)

    small_mirror_copy().wait()
    small_out.wait_send()
    small_side_copy().wait_send()
    for ahead in range(1, line):
        small_line_copy(ahead).wait_send()

    def drain(at, carry):
        pltpu.make_async_copy(unit(wide_out, at), unit(wide_out, at), out_sem.at[at]).wait()
        return carry

    lax.fori_loop(0, Exchange.UNITS, drain, 0)

    def drain_give(slot, carry):
        half_copy(slot, 0).wait_send()
        return carry

    lax.fori_loop(0, GIVE, drain_give, 0)

    def drain_wide(at, carry):
        x1(at).wait_send()
        ax(at, True).wait_send()
        return carry

    lax.fori_loop(0, wide, drain_wide, 0)
    for direction in range(2):
        rank = ranks[direction]

        def drain_line(at, carry):
            @pl.when(rank < line - 1)
            def _():
                x2(direction, at).wait_send()

            @pl.when(rank > 0)
            def _():
                a2(direction, at).wait_send()

            return carry

        lax.fori_loop(0, wide // 2, drain_line, 0)

        def drain_deep(at, carry):
            @pl.when(rank < line - 1)
            def _():
                z1(direction, at).wait_send()

            @pl.when(rank > 0)
            def _():
                a1(direction, at).wait_send()

            @pl.when((rank == line - 1) & (at % 2 != column))
            def _():
                z2(direction, at).wait_send()

            @pl.when((rank == line - 1) & (at % 2 == column))
            def _():
                a4(direction, at).wait_send()

            return carry

        lax.fori_loop(0, deep, drain_deep, 0)


def exchange(enc_operands, reg_operands, vec_grads, bias_grads, width, local, hidden):
    units, wide, deep = Exchange.UNITS, Exchange.WIDE, Exchange.DEEP
    images = len(enc_operands)

    def buffer(count, dtype=BF):
        return pltpu.VMEM((count * UNIT, width), dtype)

    def sems(*counts):
        return [pltpu.SemaphoreType.DMA((count,)) for count in counts]

    line = Exchange.LINE
    vspec = pl.BlockSpec(memory_space=pltpu.VMEM)
    return pl.pallas_call(
        functools.partial(exchange_kernel, images),
        out_shape=[
            jax.ShapeDtypeStruct((1, hidden, width), F32),
            jax.ShapeDtypeStruct((1, width, hidden), F32),
            jax.ShapeDtypeStruct((1, local, width), F32),
            jax.ShapeDtypeStruct((1, 3, width, local), F32),
            jax.ShapeDtypeStruct((16, width), F32),
            jax.ShapeDtypeStruct((16, width), F32),
        ],
        in_specs=[ANY] * (2 * images * len(OPERANDS)) + [vspec] * (2 * images),
        out_specs=[ANY] * 4 + [vspec, vspec],
        scratch_shapes=[pltpu.VMEM((images,) + one.shape, BF) for one in reg_operands[0]]
        + [
            buffer(1, F32),
            buffer(GIVE),
            buffer(units, F32),
            buffer(units),
            buffer(units),
            buffer(wide),
            buffer(wide),
            buffer(2 * deep),
            buffer(deep // 2),
            buffer(units),
            pltpu.VMEM((24, width), F32),
            pltpu.VMEM((16, width), F32),
            pltpu.VMEM((24, width), F32),
            pltpu.VMEM((16, width), F32),
            pltpu.VMEM((line, 16, width), F32),
            pltpu.SemaphoreType.DMA((len(OPERANDS), images)),
        ]
        + sems(GIVE, units, wide, wide, wide, wide, 2 * deep, 2 * deep)
        + sems(deep // 2, deep // 2, wide, wide, wide, wide, 2 * deep, 2 * deep)
        + sems(deep // 2, deep // 2, units, 3 + line, 2 + line),
        compiler_params=params_of(collective_id=0, has_side_effects=True),
        cost_estimate=pl.CostEstimate(flops=0, bytes_accessed=200_000_000, transcendentals=0),
        name="gradient_exchange",
    )(*sum(enc_operands, []), *sum(reg_operands, []), *vec_grads, *bias_grads)


def place_code(positions, model_width):
    half_width = model_width // 2
    frequency = jnp.exp(
        jnp.arange(half_width, dtype=F32) * (-math.log(10000.0) / half_width)
    )
    angles = positions.astype(F32)[..., None] * frequency
    return jnp.sin(jnp.concatenate([angles, angles + 0.5 * math.pi], -1))


def shards(
    patches,
    order,
    cotangent,
    norm_gains,
    norm_biases,
    layer_scales,
    qkv_weight,
    out_weight,
    up_weight,
    up_bias,
    down_weight,
    down_bias,
    mask_token,
):
    images, places, width = patches.shape
    rows = places // 2
    hidden = up_weight.shape[2]
    local = width // 2
    encoder = lax.axis_index("stream") == 0

    def swapped(value):
        return lax.ppermute(value, "head", SWAP)

    own = (qkv_weight[0], out_weight[0], up_weight[0], down_weight[0])
    matrices = []
    for value in own:
        matrices += [value, swapped(value)]
    bias_pair = jnp.stack([up_bias[0], swapped(up_bias[0])]).astype(F32)[:, None, :]
    vec = jnp.concatenate(
        [
            norm_gains[0],
            norm_biases[0],
            layer_scales[0],
            down_bias[0][None],
            jnp.zeros((1, width), F32),
        ]
    )
    token = mask_token[None]
    cotangent = cotangent[0]
    order_column = order[:, :, None]
    order_row = order[:, None, :]

    kept_list = list(kept_shapes(rows, rows, width, hidden).values())
    row_shape = ((rows, width), BF)
    code_shape = ((images, places, width), F32)
    grad_list = list(grad_shapes(rows, rows, width, hidden).values())
    operand_list = operand_shapes(rows, places, width, hidden)

    kept, latents = [], []
    codes = None
    for image in range(images):

        def run_encoder():
            outs = encoder_forward(
                image, 0, patches, order_column, vec, up_bias=bias_pair, matrices=matrices, save=True
            )
            return tuple(outs) + ((nothing([code_shape])[0],) if image == 0 else ())

        def run_other():
            outs = nothing([row_shape] + kept_list)
            return tuple(outs) + ((place_code(order, width),) if image == 0 else ())

        outs = lax.cond(encoder, run_encoder, run_other)
        if image == 0:
            codes = outs[-1]
            outs = outs[:-1]
        latents.append(outs[0])
        kept.append(outs[1:])
    arrived = [lax.ppermute(one, "stream", [(0, 1)]) for one in latents]

    features, returned, reg_inputs, reg_vecs, reg_biases, reg_operands = [], [], [], [], [], []
    for image in range(images):

        def run_targets():
            rest = tuple(
                nothing(
                    [row_shape, row_shape, ((places, width), F32)]
                    + [((8, width), F32), ((2, 1, hidden), F32)]
                    + operand_list
                )
            )
            if image == 0:
                rest += tuple(
                    encoder_forward(
                        None, 1, patches, order_column, vec, bias_pair, matrices, save=False
                    )
                )
            return rest

        def run_regressor():
            outs = regressor_block(
                image, arrived[image], codes, token, cotangent, vec, bias_pair, matrices
            )
            if image == 0:
                outs = tuple(outs) + tuple(nothing([((images, rows, width), BF)]))
            return tuple(outs)

        outs = lax.cond(encoder, run_targets, run_regressor)
        if image == 0:
            targets = outs[-1]
            outs = outs[:-1]
        features.append(outs[0])
        returned.append(lax.ppermute(outs[1], "stream", [(1, 0)]))
        reg_inputs.append(outs[2])
        reg_vecs.append(outs[3])
        reg_biases.append(outs[4])
        reg_operands.append(list(outs[5:]))

    input_grads, vec_grads, bias_grads, enc_operands = [], [], [], []
    for image in range(images):

        def run_backward():
            return encoder_backward(
                image, returned[image], cotangent, order_row[:, :, :rows], kept[image], vec, matrices
            )

        def run_pass():
            return (reg_inputs[image], reg_vecs[image], reg_biases[image]) + tuple(
                nothing(grad_list)
            )

        outs = lax.cond(encoder, run_backward, run_pass)
        input_grads.append(outs[0])
        vec_grads.append(outs[1])
        bias_grads.append(outs[2])
        named = dict(zip(KEPT, kept[image]))
        named.update(zip(GRADS, outs[3:]))
        enc_operands.append([named[name] for name in OPERANDS])

    if lax.axis_size("dp") == 2 * Exchange.LINE and width == 768 and hidden == 1536:
        down, up, out, qkv, totals, other = exchange(
            enc_operands, reg_operands, vec_grads, bias_grads, width, local, hidden
        )
        bias_total = totals[8 : 8 + hidden // width].reshape(hidden)
        token_grad = jnp.where(encoder, other[7], totals[7])
    else:
        parts = lax.cond(
            encoder,
            lambda: matrix_grads(enc_operands, 0),
            lambda: matrix_grads(reg_operands, rows),
        )
        vec_grad = sum(vec_grads)
        bias_grad = sum(bias_grads)[:, 0]

        def reduced(value):
            mine = value[0].astype(F32) + swapped(value[1]).astype(F32)
            part = lax.psum_scatter(mine.astype(BF), "dp", scatter_dimension=0, tiled=True)
            return lax.all_gather(part, "dp", axis=0, tiled=True).astype(F32)

        down, up, out, query, key, value = (reduced(one) for one in parts)
        qkv = jnp.stack([query, key, value])
        qkv, out, up, down = (one[None] for one in (qkv, out, up, down))
        bias_total = lax.psum(bias_grad[0] + swapped(bias_grad[1]), "dp")
        totals = lax.psum(vec_grad, ("dp", "head"))
        token_grad = lax.psum(jnp.where(encoder, 0.0, totals[7]), "stream")

    latent_out = jnp.where(encoder, jnp.stack(latents), jnp.stack(arrived))
    return (
        latent_out,
        jnp.where(encoder, targets, jnp.stack(features))[None],
        jnp.stack(input_grads)[None],
        totals[0:2][None],
        totals[2:4][None],
        totals[4:6][None],
        qkv,
        out,
        up,
        bias_total[None],
        down,
        totals[6][None],
        token_grad,
    )


def solution(mesh):
    in_specs = (
        P(("dp", "head"), None, None),
        P(("dp", "head"), None),
        P("stream", ("dp", "head"), None, None),
        P("stream", None, None),
        P("stream", None, None),
        P("stream", None, None),
        P("stream", None, None, "head"),
        P("stream", "head", None),
        P("stream", None, "head"),
        P("stream", "head"),
        P("stream", "head", None),
        P("stream", None),
        P(),
    )
    out_specs = (
        P(("dp", "head"), None, None),
        P("stream", ("dp", "head"), None, None),
        P("stream", ("dp", "head"), None, None),
        P("stream", None, None),
        P("stream", None, None),
        P("stream", None, None),
        P("stream", None, None, "head"),
        P("stream", "head", None),
        P("stream", None, "head"),
        P("stream", "head"),
        P("stream", "head", None),
        P("stream", None),
        P(),
    )
    return jax.shard_map(shards, mesh=mesh, in_specs=in_specs, out_specs=out_specs, check_vma=False)
```

profile of v0, /device:TPU:0, one launch (start us, length us, event | category | flops | bytes accessed | tf_op | source)
XLA Modules:
  0.0 348.6 jit_solution(10505435915301375929)
XLA Ops:
  0.6 0.6 collective-permute-start.3
  1.2 0.1 collective-permute-start.4
  1.3 0.4 collective-permute-start.1
  1.7 0.1 collective-permute-start.2
  1.8 0.7 reduce
  2.5 0.5 collective-permute-start
  3.0 0.9 copy.26
  3.9 0.8 concatenate.13
  4.7 7.6 %collective-permute-done = bf16[1536]{0:T(1024)(128)(2,1)S(1)} collective-permute-done((bf16[1536]{0:T(1024)(128)(2,1)S(1)}, bf16[1536]{0:T(1024)(128)(2,1)S(1)}, u32[]{:S(2)}, u32[]{:S(2)}) %collective-permute-start) | collective-permute-done | bytes 3104 | tf_op jit(solution)/shard_map/ppermute | solution.py:1340
  12.3 0.7 maximum_convert_fusion
  13.1 0.0 copy-start.1
  13.1 20.6 %conditional.6 = (bf16[256,768]{1,0:T(8,128)(2,1)}, bf16[256,768]{1,0:T(8,128)(2,1)}, bf16[256,768]{1,0:T(8,128)(2,1)}, bf16[256,768]{1,0:T(8,128)(2,1)}, bf16[2...) conditional(s32[]{:T(128)} %convert_element_type.21, ...), branch_computations={%region_0.0_spmd, %region_1.0_spmd} | conditional | flops 3825205248 | bytes 24000120 | solution.py:1381
  13.1 20.5 %encoder_forward.3 = (bf16[256,768]{1,0:T(8,128)(2,1)}, bf16[256,768]{1,0:T(8,128)(2,1)}, bf16[256,768]{1,0:T(8,128)(2,1)}, bf16[256,768]{1,0:T(8,128)(2,1)}, bf...) custom-call(bf16[2,512,768]{2,1,0:T(8,128)(2,1)} %get-tuple-element., ...), custom_call_target="tpu_custom_call" | custom-call | flops 3825205248 | bytes 24000000 | tf_op jit(solution)/shard_map/cond/branch_1_fun/encoder_forward/pallas_call | solution.py:426
  33.7 2.1 collective-permute-start.5
  35.8 20.5 %conditional.7 = (bf16[256,768]{1,0:T(8,128)(2,1)}, bf16[256,768]{1,0:T(8,128)(2,1)}, bf16[256,768]{1,0:T(8,128)(2,1)}, bf16[256,768]{1,0:T(8,128)(2,1)}, bf16[2...) conditional(s32[]{:T(128)} %convert_element_type.21, () %tuple.67, ...), branch_computations={%region_2.0_spmd.clone, %region_3.0_spmd.clone} | conditional | flops 3825205248 | bytes 26359444 | solution.py:1381
  35.8 19.8 %encoder_forward.4 = (bf16[256,768]{1,0:T(8,128)(2,1)S(1)}, bf16[256,768]{1,0:T(8,128)(2,1)}, bf16[256,768]{1,0:T(8,128)(2,1)}, bf16[256,768]{1,0:T(8,128)(2,1)}...) custom-call(bf16[2,512,768]{2,1,0:T(8,128)(2,1)} %get-tuple-element., ...), custom_call_target="tpu_custom_call" | custom-call | flops 3825205248 | bytes 24000000 | tf_op jit(solution)/shard_map/cond/branch_1_fun/encoder_forward/pallas_call | solution.py:426
  55.6 0.7 copy-done.5
  56.3 2.1 collective-permute-start.6
  58.4 30.7 %conditional.8 = (bf16[256,768]{1,0:T(8,128)(2,1)}, bf16[256,768]{1,0:T(8,128)(2,1)}, f32[512,768]{1,0:T(8,128)}, f32[8,768]{1,0:T(8,128)}, f32[2,1,1536]{2,1,0:...) conditional(s32[]{:T(128)} %convert_element_type.21, ...), branch_computations={%region_4.0_spmd, %region_5.0_spmd} | conditional | flops 9261023232 | bytes 24000128 | solution.py:1416
  58.6 30.5 %encoder_targets.1 = bf16[2,256,768]{2,1,0:T(8,128)(2,1)} custom-call(bf16[2,512,768]{2,1,0:T(8,128)(2,1)} %get-tuple-element.463.patch_ref, s32[2,512,1]{2,1,0:T(8,128)S(1)} %get-tuple-element.464.order_ref, f32[8,768]{1,0:T(8,128)S(1)} %get-tuple-element.465.vec_ref, f32[2,1,1536]{2,1,0:T(1,128)S(1)} %get-tuple-element.466.bias_ref, ...), custom_call_target="tpu_custom_call" | custom-call | flops 3825205248 | bytes 24000000 | tf_op jit(solution)/shard_map/cond/branch_1_fun/encoder_targets/pallas_call | solution.py:426
  89.1 1.3 collective-permute-start.7
  90.5 0.2 conditional.9
  90.7 0.0 copy-start.4
  90.7 1.4 collective-permute-start.8
  92.2 0.0 copy-start.2
  92.2 2.3 maximum_select_fusion
  94.5 2.1 fusion
  96.7 6.1 %collective-permute-done.7 = bf16[256,768]{1,0:T(8,128)(2,1)} collective-permute-done((bf16[256,768]{1,0:T(8,128)(2,1)}, bf16[256,768]{1,0:T(8,128)(2,1)}, u32[]{:S(2)}, u32[]{:S(2)}) %collective-permute-start.7) | collective-permute-done | bytes 393248 | tf_op jit(solution)/shard_map/ppermute | solution.py:1421
  102.7 25.7 %conditional.10 = ((f32[512,768]{1,0:T(8,128)}, f32[8,768]{1,0:T(8,128)}, f32[2,1,1536]{2,1,0:T(1,128)S(1)}, bf16[256,768]{1,0:T(8,128)(2,1)}, bf16[2,256,1536]{...) conditional(s32[]{:T(128)} %convert_element_type.21, ...), branch_computations={%region_8.0_spmd, %region_9.0_spmd} | conditional | flops 3825205248 | bytes 24004104 | solution.py:1440
  102.7 0.6 slice.18.order_ref
  103.3 25.1 %encoder_backward.2 = (f32[512,768]{1,0:T(8,128)}, f32[8,768]{1,0:T(8,128)}, f32[2,1,1536]{2,1,0:T(1,128)S(1)}, bf16[256,768]{1,0:T(8,128)(2,1)}, bf16[2,256,153...) custom-call(bf16[256,768]{1,0:T(8,128)(2,1)} %get-tuple-element.498., ...), custom_call_target="tpu_custom_call" | custom-call | flops 3825205248 | bytes 24000000 | tf_op jit(solution)/shard_map/cond/branch_1_fun/encoder_backward/pallas_call | solution.py:495
  128.5 17.5 %collective-permute-done.8 = bf16[256,768]{1,0:T(8,128)(2,1)} collective-permute-done((bf16[256,768]{1,0:T(8,128)(2,1)}, bf16[256,768]{1,0:T(8,128)(2,1)}, u32[]{:S(2)}, u32[]{:S(2)}) %collective-permute-start.8) | collective-permute-done | bytes 393248 | tf_op jit(solution)/shard_map/ppermute | solution.py:1421
  146.0 25.6 %conditional.11 = ((f32[512,768]{1,0:T(8,128)}, f32[8,768]{1,0:T(8,128)}, f32[2,1,1536]{2,1,0:T(1,128)}, bf16[256,768]{1,0:T(8,128)(2,1)}, bf16[2,256,1536]{2,1,...) conditional(s32[]{:T(128)} %convert_element_type.21, ...), branch_computations={%region_10.0_spmd, %region_11.0_spmd} | conditional | flops 3825205248 | bytes 24004104 | solution.py:1440
  146.0 0.6 slice.19.order_ref
  146.5 25.0 %encoder_backward.3 = (f32[512,768]{1,0:T(8,128)}, f32[8,768]{1,0:T(8,128)}, f32[2,1,1536]{2,1,0:T(1,128)}, bf16[256,768]{1,0:T(8,128)(2,1)}, bf16[2,256,1536]{2...) custom-call(bf16[256,768]{1,0:T(8,128)(2,1)} %get-tuple-element.532., ...), custom_call_target="tpu_custom_call" | custom-call | flops 3825205248 | bytes 24000000 | tf_op jit(solution)/shard_map/cond/branch_1_fun/encoder_backward/pallas_call | solution.py:495
  171.6 160.3 %gradient_exchange.1 = (f32[1,1536,768]{2,1,0:T(8,128)}, f32[1,768,1536]{2,1,0:T(8,128)}, f32[1,384,768]{2,1,0:T(8,128)}, f32[1,3,768,384]{3,2,1,0:T(8,128)}, f32[16,768]{1,0:T(8,128)}, /*index=5*/f32[16,768]{1,0:T(8,128)}) custom-call(bf16[256,768]{1,0:T(8,128)(2,1)} %get-tuple-element.696.refs_0_, bf16[2,256,1536]{2,1,0:T(8,128)(2,1)} %get-tuple-element.674.refs_1_, ...), custom_call_target="tpu_custom_call" | custom-call | bytes 200000000 | tf_op jit(solution)/shard_map/gradient_exchange/pallas_call | solution.py:1269
  331.9 1.5 slice_bitcast_fusion
  333.3 2.0 fusion.1
  335.3 0.6 copy.29
  335.9 1.9 maximum_bitcast_fusion
  337.8 1.3 copy-done.3
  339.0 1.8 copy.192
  340.8 1.0 copy-done.10
  341.8 1.0 copy.193
  342.9 2.4 copy.194
  345.3 0.8 slice-done
  346.1 0.3 slice-done.1
  346.4 2.2 copy.195
  (46 shorter events, 0.1 us)
Async XLA Ops:
  0.6 12.4 %collective-permute-start.3 = (bf16[768,1536]{1,0:T(8,128)(2,1)}, bf16[768,1536]{1,0:T(8,128)(2,1)S(1)}, u32[]{:S(2)}, u32[]{:S(2)}) collective-permute-start(bf16[768,1536]{1,0:T(8,128)(2,1)} %bitcast.33), channel_id=1, source_target_pairs={{0,1},{1,0},{2,3},{3,2},{4,5},{5,4},{6,7},{7,6},{8,9},{9,8},{10,11... | collective-permute-start | bytes 7077896 | tf_op jit(solution)/shard_map/ppermute | solution.py:1340
  1.2 11.9 %collective-permute-start.4 = (bf16[1536,768]{1,0:T(8,128)(2,1)}, bf16[1536,768]{1,0:T(8,128)(2,1)}, u32[]{:S(2)}, u32[]{:S(2)}) collective-permute-start(bf16[1536,768]{1,0:T(8,128)(2,1)} %bitcast.41), channel_id=1, source_target_pairs={{0,1},{1,0},{2,3},{3,2},{4,5},{5,4},{6,7},{7,6},{8,9},{9,8},{10,11... | collective-permute-start | bytes 7077896 | tf_op jit(solution)/shard_map/ppermute | solution.py:1340
  1.3 11.8 %collective-permute-start.1 = (bf16[3,768,384]{2,1,0:T(8,128)(2,1)}, bf16[3,768,384]{2,1,0:T(8,128)(2,1)}, u32[]{:S(2)}, u32[]{:S(2)}) collective-permute-start(bf16[3,768,384]{2,1,0:T(8,128)(2,1)} %bitcast.49), channel_id=1, source_target_pairs={{0,1},{1,0},{2,3},{3,2},{4,5},{5,4},{6,7},{7,6},{8,9},{9,8},{10,11... | collective-permute-start | bytes 5308424 | tf_op jit(solution)/shard_map/ppermute | solution.py:1340
  1.7 11.3 %collective-permute-start.2 = (bf16[384,768]{1,0:T(8,128)(2,1)}, bf16[384,768]{1,0:T(8,128)(2,1)S(1)}, u32[]{:S(2)}, u32[]{:S(2)}) collective-permute-start(bf16[384,768]{1,0:T(8,128)(2,1)} %bitcast.57), channel_id=1, source_target_pairs={{0,1},{1,0},{2,3},{3,2},{4,5},{5,4},{6,7},{7,6},{8,9},{9,8},{10,11... | collective-permute-start | bytes 1769480 | tf_op jit(solution)/shard_map/ppermute | solution.py:1340
  2.5 9.8 %collective-permute-start = (bf16[1536]{0:T(1024)(128)(2,1)S(1)}, bf16[1536]{0:T(1024)(128)(2,1)S(1)}, u32[]{:S(2)}, u32[]{:S(2)}) collective-permute-start(bf16[1536]{0:T(1024)(128)(2,1)S(1)} %reduce), channel_id=1, source_target_pairs={{0,1},{1,0},{2,3},{3,2},{4,5},{5,4},{6,7},{7,6},{8,9},{9,8},{10,11... | collective-permute-start | bytes 9224 | tf_op jit(solution)/shard_map/ppermute | solution.py:1340
  4.7 85.7 %copy-start.11 = (f32[8,768]{1,0:T(8,128)}, f32[8,768]{1,0:T(8,128)S(1)}, u32[]{:S(2)}) copy-start(f32[8,768]{1,0:T(8,128)S(1)} %concatenate.13) | copy-start | bytes 73732
  13.1 77.4 %copy-start.1 = (bf16[768,1536]{1,0:T(8,128)(2,1)}, bf16[768,1536]{1,0:T(8,128)(2,1)S(1)}, u32[]{:S(2)}) copy-start(bf16[768,1536]{1,0:T(8,128)(2,1)S(1)} %collective-permute-done.3) | copy-start | bytes 7077892
  33.7 24.7 %collective-permute-start.5 = (bf16[256,768]{1,0:T(8,128)(2,1)}, bf16[256,768]{1,0:T(8,128)(2,1)}, u32[]{:S(2)}, u32[]{:S(2)}) collective-permute-start(bf16[256,768]{1,0:T(8,128)(2,1)} %get-tuple-element.654), channel_id=1, source_target_pairs={{0,16},{1,17},{2,18},{3,19},{4,20},{5,21},{6,22},{7,23},{8,24},{9,... | collective-permute-start | bytes 1179656 | tf_op jit(solution)/shard_map/ppermute | solution.py:1387
  35.8 22.6 %copy-start.13 = (s32[2,512]{1,0:T(2,128)S(1)}, s32[2,512]{1,0:T(2,128)}, u32[]{:S(2)}) copy-start(s32[2,512]{1,0:T(2,128)} %param.26) | copy-start | bytes 12292
  35.8 22.6 %copy-start.14 = (f32[768]{0:T(1024)S(1)}, f32[768]{0:T(1024)}, u32[]{:S(2)}) copy-start(f32[768]{0:T(1024)} %param.37) | copy-start | bytes 9220
  55.5 0.7 copy-start.5
  56.3 2.1 copy-start.6
  56.3 34.1 %collective-permute-start.6 = (bf16[256,768]{1,0:T(8,128)(2,1)}, bf16[256,768]{1,0:T(8,128)(2,1)}, u32[]{:S(2)}, u32[]{:S(2)}) collective-permute-start(bf16[256,768]{1,0:T(8,128)(2,1)} %get-tuple-element.655), channel_id=1, source_target_pairs={{0,16},{1,17},{2,18},{3,19},{4,20},{5,21},{6,22},{7,23},{8,24},{9,... | collective-permute-start | bytes 1179656 | tf_op jit(solution)/shard_map/ppermute | solution.py:1387
  89.1 13.6 %collective-permute-start.7 = (bf16[256,768]{1,0:T(8,128)(2,1)}, bf16[256,768]{1,0:T(8,128)(2,1)}, u32[]{:S(2)}, u32[]{:S(2)}) collective-permute-start(bf16[256,768]{1,0:T(8,128)(2,1)} %get-tuple-element.663), channel_id=1, source_target_pairs={{16,0},{17,1},{18,2},{19,3},{20,4},{21,5},{22,6},{23,7},{24,8},{25... | collective-permute-start | bytes 1179656 | tf_op jit(solution)/shard_map/ppermute | solution.py:1421
  90.5 1.7 copy-start.7
  90.7 3.8 %copy-start.4 = (bf16[2,256,768]{2,1,0:T(8,128)(2,1)S(1)}, bf16[2,256,768]{2,1,0:T(8,128)(2,1)}, u32[]{:S(2)}) copy-start(bf16[2,256,768]{2,1,0:T(8,128)(2,1)} %get-tuple-element.657) | copy-start | bytes 2359300
  90.7 3.8 %copy-start.12 = (bf16[256,768]{1,0:T(8,128)(2,1)S(1)}, bf16[256,768]{1,0:T(8,128)(2,1)}, u32[]{:S(2)}) copy-start(bf16[256,768]{1,0:T(8,128)(2,1)} %get-tuple-element.658) | copy-start | bytes 1179652
  90.7 55.2 %collective-permute-start.8 = (bf16[256,768]{1,0:T(8,128)(2,1)}, bf16[256,768]{1,0:T(8,128)(2,1)}, u32[]{:S(2)}, u32[]{:S(2)}) collective-permute-start(bf16[256,768]{1,0:T(8,128)(2,1)} %get-tuple-element.917), channel_id=1, source_target_pairs={{16,0},{17,1},{18,2},{19,3},{20,4},{21,5},{22,6},{23,7},{24,8},{25... | collective-permute-start | bytes 1179656 | tf_op jit(solution)/shard_map/ppermute | solution.py:1421
  92.2 10.5 %copy-start.2 = (bf16[1,384,768]{2,1,0:T(8,128)(2,1)S(1)}, bf16[1,384,768]{2,1,0:T(8,128)(2,1)}, u32[]{:S(2)}) copy-start(bf16[1,384,768]{2,1,0:T(8,128)(2,1)} %param.32) | copy-start | bytes 1769476
  94.5 8.2 %copy-start = (bf16[1,768,1536]{2,1,0:T(8,128)(2,1)S(1)}, bf16[1,768,1536]{2,1,0:T(8,128)(2,1)}, u32[]{:S(2)}) copy-start(bf16[1,768,1536]{2,1,0:T(8,128)(2,1)} %param.33) | copy-start | bytes 7077892
  171.5 164.4 %copy-start.8 = (f32[512,768]{1,0:T(8,128)S(1)}, f32[512,768]{1,0:T(8,128)}, u32[]{:S(2)}) copy-start(f32[512,768]{1,0:T(8,128)} %get-tuple-element.677) | copy-start | bytes 4718596
  171.5 164.4 %copy-start.9 = (f32[512,768]{1,0:T(8,128)S(1)}, f32[512,768]{1,0:T(8,128)}, u32[]{:S(2)}) copy-start(f32[512,768]{1,0:T(8,128)} %get-tuple-element.695) | copy-start | bytes 4718596
  335.9 3.1 copy-start.3
  335.9 7.0 %slice-start.2 = ((s8[4718592]{0:T(1024)(128)(4,1)}), s8[4194304]{0:T(1024)(128)(4,1)S(1)}, s32[]{:S(2)}) async-start(s8[4718592]{0:T(1024)(128)(4,1)} %bitcast.67), calls=%async_computation.2 | async-start | bytes 8388608
  339.0 2.8 copy-start.10
  339.0 3.8 %slice-start.3 = ((s8[4718592]{0:T(1024)(128)(4,1)}), s8[524288]{0:T(1024)(128)(4,1)S(1)}, s32[]{:S(2)}) async-start(s8[4718592]{0:T(1024)(128)(4,1)} %bitcast.67), calls=%async_computation.3 | async-start | bytes 1048576
  341.8 4.3 %slice-start = ((s8[4718592]{0:T(1024)(128)(4,1)}), s8[4194304]{0:T(1024)(128)(4,1)S(1)}, s32[]{:S(2)}) async-start(s8[4718592]{0:T(1024)(128)(4,1)} %bitcast.65), calls=%async_computation | async-start | bytes 8388608
  342.9 3.5 %slice-start.1 = ((s8[4718592]{0:T(1024)(128)(4,1)}), s8[524288]{0:T(1024)(128)(4,1)S(1)}, s32[]{:S(2)}) async-start(s8[4718592]{0:T(1024)(128)(4,1)} %bitcast.65), calls=%async_computation.1 | async-start | bytes 1048576
where the time goes:
time: 349 us
  Pallas kernels  281 us (81%)
  waiting for transfers between devices  31.2 us (9%)
  local copies, waits for them, and re-layouts  16.5 us (5%)
  other arithmetic  9.73 us (3%)
  starting transfers between devices  8.52 us (2%)
    pallas_call x1, Pallas kernels, exchange(): pl.pallas_call(functools.partial(exchange_kernel, images), out_shape=[jax...  160 us
    pallas_call x3, Pallas kernels, encoder_forward(): pl.pallas_call(kernel, grid=(1 if save else images,), out_shape=[shape_of...  70.8 us
    pallas_call x2, Pallas kernels, encoder_backward(): pl.pallas_call(kernel, grid=(1,), out_shape=[shape_of(s) for s in out_sha...  50.1 us
    ppermute x2, waiting for transfers between devices, shards(): returned.append(lax.ppermute(outs[1], 'stream', [(1, 0)]))  23.6 us
    unnamed x42, local copies, waits for them, and re-layouts  12.9 us
    ppermute x5, waiting for transfers between devices, swapped(): return lax.ppermute(value, 'head', SWAP)  7.64 us
  transfers between devices with their start and end apart: 9, of which 3 were waited for; matrix products, arithmetic and copies ran while one was open for 2% of the time, Pallas kernels for 22%

commit v1 on v0

--- a/solution.py
+++ b/solution.py
@@ -103,6 +103,35 @@
         return self.buffers[name]
 
 
+class Held(dict):
+    def __init__(self, buffers):
+        super().__init__(buffers)
+        self.coming, self.going = {}, {}
+
+    def copy_in(self, names, sources, sems):
+        for at, (name, source) in enumerate(zip(names, sources)):
+            self.coming[name] = pltpu.make_async_copy(source, self[name], sems.at[at])
+            self.coming[name].start()
+
+    def copy_out(self, names, targets, sems):
+        for at, (name, target) in enumerate(zip(names, targets)):
+            self.going[name] = pltpu.make_async_copy(self[name], target, sems.at[at])
+
+    def need(self, *names):
+        for name in names:
+            if name in self.coming:
+                self.coming[name].wait()
+
+    def ready(self, *names):
+        for name in names:
+            if name in self.going:
+                self.going[name].start()
+
+    def finish(self):
+        for copy in self.going.values():
+            copy.wait()
+
+
 def weight_scratch(width, local, hidden):
     return [
         pltpu.VMEM((2, 3, width, local), BF),
@@ -126,6 +155,7 @@
         keep[name] for name in ("N", "Q", "K", "V", "P", "O")
     )
     norm_into(rows_all, normed, vec[0:1, :], vec[2:3, :])
+    keep.ready("N")
     weights.wait("qkv")
     local = weights["qkv"].shape[3]
 
@@ -135,6 +165,7 @@
         values[:, cols] = dot(normed[...], weights["qkv"][half, 2]).astype(BF)
 
     halves_loop(local, project)
+    keep.ready("Q", "K", "V")
     masks = head_masks()
 
     def attend(pair, carry):
@@ -152,12 +183,14 @@
         return carry
 
     lax.fori_loop(0, HEADS // 2, attend, 0)
+    keep.ready("P", "O")
     weights.wait("out")
     attended = dot(mixed[:, :local], weights["out"][0]) + dot(mixed[:, local:], weights["out"][1])
     hidden, normed_two = keep["H"], keep["M"]
     keep["A"][...] = attended.astype(keep["A"].dtype)
     hidden[...] = rows_all[ctx:, :] + vec[4:5, :] * attended
     norm_into(hidden, normed_two, vec[1:2, :], vec[3:4, :])
+    keep.ready("A", "H", "M")
     weights.wait("up")
     weights.wait("down")
     fed = keep["F"]
@@ -180,6 +213,8 @@
 
     lax.fori_loop(0, 2 * per_half, feed, 0)
 
+    keep.ready("G", "D", "F")
+
     def finish(rows):
         result_fn(rows, hidden[rows, :] + vec[5:6, :] * fed[rows, :])
 
@@ -202,7 +237,10 @@
         sums[6] += fold_rows(branch)
         grads["dF"][rows, :] = branch.astype(BF)
 
+    keep.need("F")
     row_loop(row_count, enter)
+    grads.ready("dF")
+    keep.need("D")
     weights.wait("down")
     weights.wait("up")
     grad_mid = work["dM"]
@@ -233,7 +271,10 @@
         sums[4] += fold_rows(hidden_grad * keep["A"][rows, :].astype(F32))
         grads["dA"][rows, :] = (vec[4:5, :] * hidden_grad).astype(BF)
 
+    grads.ready("dU")
+    keep.need("H", "A")
     row_loop(row_count, middle)
+    grads.ready("dA")
     weights.wait("out")
     mix_grad = work["dO"]
 
@@ -267,7 +308,9 @@
         grads["dQ"][:, cols] = (jnp.concatenate(query_grads, 0).T * 0.125).astype(BF)
         return carry
 
+    keep.need("P", "Q", "K", "V")
     lax.fori_loop(0, HEADS // 2, attend, 0)
+    grads.ready("dQ", "dK", "dV")
     weights.wait("qkv")
     grad_all = work["dN"]
     qkv = weights["qkv"]
@@ -282,12 +325,13 @@
     halves_loop(local, unproject)
 
     def leave(rows):
-        scaled, inv_std = standardize(rows_all[rows, :])
+        scaled, inv_std = standardize(rows_all[rows, :].astype(F32))
         grad = grad_all[rows, :]
         sums[0] += fold_rows(grad * scaled)
         sums[2] += fold_rows(grad)
         grad_all[rows, :] = norm_back(grad, scaled, inv_std, vec[0:1, :])
 
+    keep.need("X")
     row_loop(rows_all.shape[0], leave)
 
 
@@ -301,6 +345,7 @@
     return dot((places == order_column).astype(F32).astype(BF), patches)
 
 
+READ_BACK = ("F", "D", "H", "A", "P", "Q", "K", "V", "X")
 KEPT = ("X", "N", "Q", "K", "V", "P", "O", "A", "H", "M", "G", "D", "F")
 GRADS = ("dF", "dU", "dA", "dQ", "dK", "dV")
 OPERANDS = ("dF", "G", "dU", "M", "dA", "O", "dQ", "dK", "dV", "N")
@@ -387,34 +432,35 @@
     local = width // 2
     shapes = kept_shapes(rows, rows, width, hidden)
     names = [n for n in KEPT]
+    own = names if save else [n for n in names if n not in ("X", "G", "D")]
 
     def kernel(patch_ref, order_ref, vec_ref, bias_ref, *refs):
         sources, refs = refs[:8], refs[8:]
         result, refs = refs[0], refs[1:]
         if save:
-            keep = dict(zip(names, refs[: len(names)]))
-            refs = refs[len(names) :]
-        else:
-            own = [n for n in names if n not in ("X", "G", "D")]
-            keep = dict(zip(own, refs[: len(own)]))
-            refs = refs[len(own) :]
+            targets, refs = refs[: len(names)], refs[len(names) :]
+        keep = Held(zip(own, refs))
+        refs = refs[len(own) :]
         rows_ref, refs = refs[0], refs[1:]
         weights = Weights(sources, refs[:4], refs[4], first_only=not save)
         weights.start(("qkv", "out", "up", "down"))
         rows_ref[...] = pick_rows(order_ref[...], patch_ref[...])
         if save:
+            keep.copy_out(names, targets, refs[5])
             keep["X"][...] = rows_ref[...].astype(BF)
+            keep.ready("X")
 
         def result_fn(rows_at, value):
             result[rows_at, :] = value.astype(BF)
 
         forward(rows_ref, 0, vec_ref, bias_ref, weights, keep, result_fn)
+        keep.finish()
 
     out_shapes = [((rows, width), BF)] + ([shapes[n] for n in names] if save else [])
-    out_specs = [whole(s[0]) for s in out_shapes]
+    out_specs = [whole(out_shapes[0][0])] + [ANY] * (len(out_shapes) - 1)
     patch_spec = image_of(patches, image)
-    scratch = [] if save else [vmem(shapes[n]) for n in names if n not in ("X", "G", "D")]
-    scratch = scratch + [pltpu.VMEM((rows, width), F32)] + weight_scratch(width, local, hidden)
+    scratch = [vmem(shapes[n]) for n in own] + [pltpu.VMEM((rows, width), F32)]
+    scratch += weight_scratch(width, local, hidden) + [pltpu.SemaphoreType.DMA((len(names),))]
     order_spec = pl.BlockSpec(
         (None, rows, 1), lambda _: (image, which, 0), pipeline_mode=ONCE
     )
@@ -442,24 +488,31 @@
     local = width // 2
     shapes = grad_shapes(rows, rows, width, hidden)
     names = list(GRADS)
+    kept = [dict(zip(KEPT, kept))[name] for name in READ_BACK]
 
     def kernel(back_ref, cot_ref, order_ref, vec_ref, *refs):
         sources, refs = refs[:8], refs[8:]
-        keep = dict(zip(KEPT, refs[: len(KEPT)]))
-        refs = refs[len(KEPT) :]
+        saved, refs = refs[: len(READ_BACK)], refs[len(READ_BACK) :]
         input_grad, vec_grad, bias_grad, refs = refs[0], refs[1], refs[2], refs[3:]
-        grads = dict(zip(names, refs[: len(names)]))
-        refs = refs[len(names) :]
-        rows_ref, d_hidden, d_mid, d_out, d_norm, sums = refs[:6]
-        weights = Weights(sources, refs[6:10], refs[10])
-        weights.start(("down", "up", "out", "qkv"))
+        targets, refs = refs[: len(names)], refs[len(names) :]
+        keep = Held(zip(READ_BACK, refs))
+        grads = Held(zip(names, refs[len(READ_BACK) :]))
+        refs = refs[len(READ_BACK) + len(names) :]
+        d_hidden, d_mid, d_out, d_norm, sums = refs[:5]
+        weights = Weights(sources, refs[5:9], refs[9])
+        keep.copy_in(READ_BACK[:2], saved, refs[11])
+        weights.start(("down", "up"))
+        keep.copy_in(READ_BACK[2:], saved[2:], refs[12])
+        weights.start(("out", "qkv"))
+        grads.copy_out(names, targets, refs[13])
         work = {"dH": d_hidden, "dM": d_mid, "dO": d_out, "dN": d_norm}
-        rows_ref[...] = keep["X"][...].astype(F32)
 
         def out_grad_fn(rows_at):
             return cot_ref[rows_at, :].astype(F32) + back_ref[rows_at, :].astype(F32)
 
-        backward(rows_ref, 0, out_grad_fn, vec_ref, weights, keep, grads, work, sums, bias_grad)
+        backward(
+            keep["X"], 0, out_grad_fn, vec_ref, weights, keep, grads, work, sums, bias_grad
+        )
         write_sums(sums, vec_grad)
 
         def join(rows_at):
@@ -468,7 +521,7 @@
             d_out[rows_at, :] = high
             grads_low[rows_at, :] = (total - high.astype(F32)).astype(BF)
 
-        grads_low = refs[11]
+        grads_low = refs[10]
         row_loop(rows, join)
 
         def place(index, carry):
@@ -479,11 +532,13 @@
             return carry
 
         lax.fori_loop(0, input_grad.shape[0] // 128, place, 0)
+        grads.finish()
 
     out_shapes = [((2 * rows, width), F32), ((8, width), F32), ((2, 1, hidden), F32)]
     out_shapes += [shapes[n] for n in names]
-    scratch = [
-        pltpu.VMEM((rows, width), F32),
+    forms = kept_shapes(rows, rows, width, hidden)
+    scratch = [vmem(forms[n]) for n in READ_BACK] + [vmem(shapes[n]) for n in names]
+    scratch += [
         pltpu.VMEM((rows, width), F32),
         pltpu.VMEM((rows, width), F32),
         pltpu.VMEM((rows, width), BF),
@@ -491,15 +546,19 @@
         pltpu.VMEM((8, 8, width), F32),
     ]
     scratch += weight_scratch(width, local, hidden) + [pltpu.VMEM((rows, width), BF)]
+    scratch += [
+        pltpu.SemaphoreType.DMA((2,)),
+        pltpu.SemaphoreType.DMA((len(READ_BACK) - 2,)),
+        pltpu.SemaphoreType.DMA((len(names),)),
+    ]
     order_spec = pl.BlockSpec((None, 1, rows), lambda _: (image, 0, 0), pipeline_mode=ONCE)
     outs = pl.pallas_call(
         kernel,
         grid=(1,),
         out_shape=[shape_of(s) for s in out_shapes],
         in_specs=[whole(latent_grad.shape), image_of(cotangent, image), order_spec, whole(vec.shape)]
-        + [ANY] * 8
-        + [whole(k.shape) for k in kept],
-        out_specs=[whole(s[0]) for s in out_shapes],
+        + [ANY] * (8 + len(kept)),
+        out_specs=[whole(s[0]) for s in out_shapes[:3]] + [ANY] * len(names),
         scratch_shapes=scratch,
         compiler_params=params_of(),
         cost_estimate=block_cost(rows, rows, width, hidden, 1),
@@ -528,11 +587,11 @@
         sources, refs = refs[:8], refs[8:]
         result, back, input_grad, vec_grad, bias_grad = refs[:5]
         refs = refs[5:]
-        named = dict(zip(OPERANDS, refs[: len(OPERANDS)]))
-        refs = refs[len(OPERANDS) :]
-        keep = dict(named)
-        keep.update(zip(own, refs[: len(own)]))
-        refs = refs[len(own) :]
+        targets, refs = refs[: len(OPERANDS)], refs[len(OPERANDS) :]
+        held = OPERANDS + tuple(own)
+        keep = Held(zip(held, refs))
+        refs = refs[len(held) :]
+        keep.copy_out(OPERANDS, targets, refs[10])
         rows_ref, d_hidden, d_mid, d_out, sums = refs[:5]
         weights = Weights(sources, refs[5:9], refs[9])
         weights.start(("qkv", "out", "up", "down"))
@@ -555,7 +614,7 @@
 
         weights.wait = lambda name: None
         backward(
-            rows_ref, ctx, out_grad_fn, vec_ref, weights, keep, named, work, sums, bias_grad
+            rows_ref, ctx, out_grad_fn, vec_ref, weights, keep, keep, work, sums, bias_grad
         )
 
         def leave(rows_at):
@@ -567,6 +626,7 @@
 
         row_loop(rows, leave)
         write_sums(sums, vec_grad)
+        keep.finish()
 
     out_shapes = [
         ((rows, width), BF),
@@ -575,7 +635,8 @@
         ((8, width), F32),
         ((2, 1, hidden), F32),
     ] + operand_shapes(rows, keys, width, hidden)
-    scratch = [vmem(kept[n]) for n in own]
+    scratch = [vmem(one) for one in operand_shapes(rows, keys, width, hidden)]
+    scratch += [vmem(kept[n]) for n in own]
     scratch += [
         pltpu.VMEM((keys, width), F32),
         pltpu.VMEM((rows, width), F32),
@@ -584,6 +645,7 @@
         pltpu.VMEM((8, 8, width), F32),
     ]
     scratch += weight_scratch(width, local, hidden)
+    scratch += [pltpu.SemaphoreType.DMA((len(OPERANDS),))]
     outs = pl.pallas_call(
         kernel,
         grid=(1,),
@@ -597,7 +659,7 @@
             whole(up_bias.shape),
         ]
         + [ANY] * 8,
-        out_specs=[whole(s[0]) for s in out_shapes],
+        out_specs=[whole(s[0]) for s in out_shapes[:5]] + [ANY] * len(OPERANDS),
         scratch_shapes=scratch,
         compiler_params=params_of(),
         cost_estimate=block_cost(rows, keys, width, hidden, 2),
@@ -675,13 +737,13 @@
 
 UNIT = 128
 LAG = 2
-GIVE = 8
+GIVE = 16
 
 
 class Exchange:
     LINE = 4
-    WIDE = 10
-    DEEP = 8
+    WIDE = 20
+    DEEP = 16
     UNITS = 2 * WIDE + 2 * DEEP
 
 
@@ -696,8 +758,8 @@
     totals_ref, other_ref = refs[4:6]
     refs = refs[6:]
     held = dict(zip(OPERANDS, refs[:count]))
-    acc, gives, wide_out = refs[count : count + 3]
-    refs = refs[count + 3 :]
+    acc, gives = refs[count : count + 2]
+    refs = refs[count + 2 :]
     total, own_half, from_column, from_line, from_deep, from_side, done = refs[:7]
     small_ref, small_own, small_half, small_side, small_line = refs[7:12]
     (load_sem, half_send, half_recv, x1_send, x1_recv, x2_send, x2_recv, z1_send, z1_recv) = refs[12:21]
@@ -773,11 +835,15 @@
     small_out = remote(small_ref, small_half, s_send.at[1], s_recv.at[0], partner)
     small_out.start()
 
-    first_up = hidden // UNIT
-    first_out = 2 * first_up
-    first_pair = first_out + local // UNIT
-    first_query = first_pair + width // UNIT
-    bounds = (0, first_up, first_out, first_pair, first_query, Exchange.UNITS)
+    counts = (
+        2 * hidden // UNIT,
+        2 * hidden // UNIT,
+        2 * local // UNIT,
+        width // UNIT,
+        width // UNIT,
+        width // UNIT,
+    )
+    bounds = [sum(counts[:at]) for at in range(len(counts) + 1)]
 
     def by_kind(at, bodies):
         for kind, one in enumerate(bodies):
@@ -794,12 +860,16 @@
         return functools.reduce(jnp.add, parts)
 
     def product(at, half):
-        cols = slice(half * local, (half + 1) * local)
+        cols = pl.ds(pl.multiple_of(half * local, local), local)
         query_rows = pl.ds(pl.multiple_of(stream * rows, rows), rows)
 
         def down(index):
             acc[...] = summed(
-                lambda i: dot(held["G"][i, half, :, block(index)], held["dF"][i], TN)
+                lambda i: dot(
+                    held["G"][i, half, :, block(index // 2)],
+                    held["dF"][i, :, block(index % 2, local)],
+                    TN,
+                )
             )
 
         def up(index):
@@ -807,7 +877,7 @@
             acc[...] = summed(
                 lambda i: dot(
                     held["M"][i, :, block(index % per)],
-                    held["dU"][i, half, :, block(index // per, width)],
+                    held["dU"][i, half, :, block(index // per, local)],
                     TN,
                 )
             )
@@ -815,35 +885,33 @@
         def out(index):
             acc[...] = summed(
                 lambda i: dot(
-                    held["O"][i, :, block(half * (local // UNIT) + index)], held["dA"][i], TN
+                    held["O"][i, :, block(half * (local // UNIT) + index // 2)],
+                    held["dA"][i, :, block(index % 2, local)],
+                    TN,
                 )
             )
 
-        def pair(index):
-            def part(name, keys):
+        def over_keys(name):
+            def part(index, keys):
                 return summed(
                     lambda i: dot(held["N"][i, keys, block(index)], held[name][i, keys, cols], TN)
                 )
 
-            acc[:, :local] = part("dK", slice(0, rows))
-            acc[:, local:] = part("dV", slice(0, rows))
-
-            @pl.when(stream == 1)
-            def _():
-                acc[:, :local] += part("dK", slice(rows, None))
-                acc[:, local:] += part("dV", slice(rows, None))
+            def run(index):
+                acc[...] = part(index, slice(0, rows))
+
+                @pl.when(stream == 1)
+                def _():
+                    acc[...] += part(index, slice(rows, None))
+
+            return run
 
         def query(index):
-            for at in range(2):
-                acc[:, at * local : (at + 1) * local] = summed(
-                    lambda i: dot(
-                        held["N"][i, query_rows, block(at * (local // UNIT) + index)],
-                        held["dQ"][i, :, cols],
-                        TN,
-                    )
-                )
-
-        by_kind(at, (down, up, out, pair, query))
+            acc[...] = summed(
+                lambda i: dot(held["N"][i, query_rows, block(index)], held["dQ"][i, :, cols], TN)
+            )
+
+        by_kind(at, (down, up, out, over_keys("dK"), over_keys("dV"), query))
 
     def chunks(body):
         def step(index, carry):
@@ -863,62 +931,57 @@
         wide_unit = 2 * step + 1 - column + own * (2 * column - 1)
         return wide_unit + second * (2 * wide + 2 * step + own - wide_unit), second
 
-    def make_give(step):
-        def body(index, carry):
-            at, second = unit_of(step, index)
-
-            @pl.when((step < wide) & (second * step < deep))
-            def _():
-                slot = (4 * step + index) % GIVE
-
-                @pl.when(4 * step >= GIVE)
-                def _():
-                    half_copy(slot, at).wait_send()
-
-                product(at, 1)
-
-                def convert(offset):
-                    gives[pl.ds(pl.multiple_of(slot * UNIT + offset, 32), 32), :] = acc[
-                        pl.ds(offset, 32), :
-                    ].astype(BF)
-
-                chunks(convert)
-                half_copy(slot, at).start()
-
-            return carry
-
-        lax.fori_loop(0, 4, body, 0)
-
-    def make_own(step):
-        def body(index, carry):
+    def make(now):
+        def body(turn, carry):
+            index, mine = turn % 4, turn // 4
+            step = now + 1 - mine
             at, second = unit_of(step, index)
 
             @pl.when((step >= 0) & (step < wide) & (second * step < deep))
             def _():
-                product(at, 0)
-                half_copy(0, at).wait_recv()
-
-                def join(offset):
-                    where = pl.ds(pl.multiple_of(at * UNIT + offset, 32), 32)
-                    total[where, :] = (
-                        acc[pl.ds(offset, 32), :] + own_half[where, :].astype(F32)
-                    ).astype(BF)
-
-                chunks(join)
-
-                @pl.when(index == 0)
+                product(at, 1 - mine)
+
+                @pl.when(mine == 0)
                 def _():
-                    x1(step).start()
-
-                for direction in range(2):
-
-                    @pl.when((index == 1 + direction) & (ranks[direction] == 0))
+                    slot = (4 * step + index) % GIVE
+
+                    @pl.when(4 * step >= GIVE)
                     def _():
-                        z1(direction, step).start()
+                        half_copy(slot, at).wait_send()
+
+                    def convert(offset):
+                        gives[pl.ds(pl.multiple_of(slot * UNIT + offset, 32), 32), :] = acc[
+                            pl.ds(offset, 32), :
+                        ].astype(BF)
+
+                    chunks(convert)
+                    half_copy(slot, at).start()
+
+                @pl.when(mine == 1)
+                def _():
+                    half_copy(0, at).wait_recv()
+
+                    def join(offset):
+                        where = pl.ds(pl.multiple_of(at * UNIT + offset, 32), 32)
+                        total[where, :] = (
+                            acc[pl.ds(offset, 32), :] + own_half[where, :].astype(F32)
+                        ).astype(BF)
+
+                    chunks(join)
+
+                    @pl.when(index == 0)
+                    def _():
+                        x1(step).start()
+
+                    for direction in range(2):
+
+                        @pl.when((index == 1 + direction) & (ranks[direction] == 0))
+                        def _():
+                            z1(direction, step).start()
 
             return carry
 
-        lax.fori_loop(0, 4, body, 0)
+        lax.fori_loop(0, 8, body, 0)
 
     def add(target, at, first, first_at, second, second_at):
         def body(index, carry):
@@ -989,39 +1052,20 @@
         return finished(2 * wide + 2 * at + direction, a4_send, a4_recv, at // 2, side)
 
     def put(at):
-        def widen(offset):
-            where = pl.ds(pl.multiple_of(at * UNIT + offset, 32), 32)
-            wide_out[where, :] = done[where, :].astype(F32)
-
-        chunks(widen)
-
-        def send(target, cols=slice(None)):
-            pltpu.make_async_copy(unit(wide_out, at).at[:, cols], target, out_sem.at[at]).start()
-
-        left, right = pl.ds(0, local), pl.ds(local, local)
+        def send(target):
+            pltpu.make_async_copy(unit(done, at), target, out_sem.at[at]).start()
+
+        def by_rows(ref):
+            return lambda index: send(ref.at[block(index // 2), block(index % 2, local)])
 
         def up(index):
             per = width // UNIT
-            send(up_ref.at[block(index % per), block(index // per, width)])
-
-        def pair(index):
-            send(qkv_ref.at[1, block(index), :], left)
-            send(qkv_ref.at[2, block(index), :], right)
-
-        def query(index):
-            send(qkv_ref.at[0, block(index), :], left)
-            send(qkv_ref.at[0, block(local // UNIT + index), :], right)
-
-        by_kind(
-            at,
-            (
-                lambda index: send(down_ref.at[block(index), :]),
-                up,
-                lambda index: send(out_ref.at[block(index), :]),
-                pair,
-                query,
-            ),
-        )
+            send(up_ref.at[block(index % per), block(index // per, local)])
+
+        def part(which):
+            return lambda index: send(qkv_ref.at[which, block(index), :])
+
+        by_kind(at, (by_rows(down_ref), up, by_rows(out_ref), part(1), part(2), part(0)))
 
     def small_phase(step):
         @pl.when(step == 2)
@@ -1067,12 +1111,11 @@
         )
 
     def step_body(step, carry):
-        @pl.when(step == 1)
+        @pl.when(step == 3)
         def _():
             load(rest, "wait")
 
-        make_give(step + 1)
-        make_own(step)
+        make(step)
 
         at = step - LAG
 
@@ -1199,7 +1242,7 @@
         small_line_copy(ahead).wait_send()
 
     def drain(at, carry):
-        pltpu.make_async_copy(unit(wide_out, at), unit(wide_out, at), out_sem.at[at]).wait()
+        pltpu.make_async_copy(unit(done, at), unit(done, at), out_sem.at[at]).wait()
         return carry
 
     lax.fori_loop(0, Exchange.UNITS, drain, 0)
@@ -1259,7 +1302,7 @@
     images = len(enc_operands)
 
     def buffer(count, dtype=BF):
-        return pltpu.VMEM((count * UNIT, width), dtype)
+        return pltpu.VMEM((count * UNIT, local), dtype)
 
     def sems(*counts):
         return [pltpu.SemaphoreType.DMA((count,)) for count in counts]
@@ -1269,10 +1312,10 @@
     return pl.pallas_call(
         functools.partial(exchange_kernel, images),
         out_shape=[
-            jax.ShapeDtypeStruct((1, hidden, width), F32),
-            jax.ShapeDtypeStruct((1, width, hidden), F32),
-            jax.ShapeDtypeStruct((1, local, width), F32),
-            jax.ShapeDtypeStruct((1, 3, width, local), F32),
+            jax.ShapeDtypeStruct((1, hidden, width), BF),
+            jax.ShapeDtypeStruct((1, width, hidden), BF),
+            jax.ShapeDtypeStruct((1, local, width), BF),
+            jax.ShapeDtypeStruct((1, 3, width, local), BF),
             jax.ShapeDtypeStruct((16, width), F32),
             jax.ShapeDtypeStruct((16, width), F32),
         ],
@@ -1282,7 +1325,6 @@
         + [
             buffer(1, F32),
             buffer(GIVE),
-            buffer(units, F32),
             buffer(units),
             buffer(units),
             buffer(wide),
@@ -1449,6 +1491,7 @@
         down, up, out, qkv, totals, other = exchange(
             enc_operands, reg_operands, vec_grads, bias_grads, width, local, hidden
         )
+        down, up, out, qkv = (one.astype(F32) for one in (down, up, out, qkv))
         bias_total = totals[8 : 8 + hidden // width].reshape(hidden)
         token_grad = jnp.where(encoder, other[7], totals[7])
     else:

time: 349 us -> 340 us (0.974)
  other arithmetic: 9.73 us -> 19.4 us
  local copies, waits for them, and re-layouts: 16.5 us -> 7.23 us
  Pallas kernels: 281 us -> 272 us
    convert_element_type x0 -> x4, other arithmetic: none -> 9.62 us  [shards(): down, up, out, qkv = (one.astype(F32) for one in (down, up, out, qkv))]
    unnamed x42 -> x32, local copies, waits for them, and re-layouts: 12.9 us -> 3.66 us
  transfers between devices with their start and end apart: 9 -> 9, of which waited for: 3 -> 3; matrix products, arithmetic and copies ran while one was open for 2% -> 2% of each run, Pallas kernels for 22% -> 21%
where the time goes in v1:
time: 340 us; the launch traced here: 339 us
  Pallas kernels  272 us (80%)
  waiting for transfers between devices  30.9 us (9%)
  other arithmetic  19.4 us (6%)
  starting transfers between devices  8.44 us (2%)
  local copies, waits for them, and re-layouts  7.23 us (2%)
    pallas_call x1, Pallas kernels, exchange(): pl.pallas_call(functools.partial(exchange_kernel, images), out_shape=[jax...  157 us
    pallas_call x3, Pallas kernels, encoder_forward(): pl.pallas_call(kernel, grid=(1 if save else images,), out_shape=[shape_of...  67.9 us
    pallas_call x2, Pallas kernels, encoder_backward(): pl.pallas_call(kernel, grid=(1,), out_shape=[shape_of(s) for s in out_sha...  46.7 us
    ppermute x2, waiting for transfers between devices, shards(): returned.append(lax.ppermute(outs[1], 'stream', [(1, 0)]))  23.3 us
    convert_element_type x4, other arithmetic, shards(): down, up, out, qkv = (one.astype(F32) for one in (down, up, out, qkv))  9.62 us
    ppermute x5, waiting for transfers between devices, swapped(): return lax.ppermute(value, 'head', SWAP)  7.64 us
  transfers between devices with their start and end apart: 9, of which 3 were waited for; matrix products, arithmetic and copies ran while one was open for 2% of the time, Pallas kernels for 21%

profile of v1, /device:TPU:0, one launch (start us, length us, event | category | flops | bytes accessed | tf_op | source)
XLA Modules:
  0.0 339.2 jit_solution(7455958282931151122)
XLA Ops:
  0.6 0.6 collective-permute-start.3
  1.2 0.1 collective-permute-start.4
  1.3 0.4 collective-permute-start.1
  1.7 0.1 collective-permute-start.2
  1.8 0.7 reduce
  2.5 0.5 collective-permute-start
  3.0 0.9 copy.26
  3.9 0.8 concatenate.13
  4.7 7.6 %collective-permute-done = bf16[1536]{0:T(1024)(128)(2,1)S(1)} collective-permute-done((bf16[1536]{0:T(1024)(128)(2,1)S(1)}, bf16[1536]{0:T(1024)(128)(2,1)S(1)}, u32[]{:S(2)}, u32[]{:S(2)}) %collective-permute-start) | collective-permute-done | bytes 3104 | tf_op jit(solution)/shard_map/ppermute | solution.py:1382
  12.3 0.7 maximum_convert_fusion
  13.0 0.0 collective-permute-done.2
  13.1 0.0 copy-start.1
  13.1 19.3 %conditional.6 = (bf16[256,768]{1,0:T(8,128)(2,1)}, bf16[256,768]{1,0:T(8,128)(2,1)}, bf16[256,768]{1,0:T(8,128)(2,1)}, bf16[256,768]{1,0:T(8,128)(2,1)}, bf16[2...) conditional(s32[]{:T(128)} %convert_element_type.33, ...), branch_computations={%region_0.0_spmd, %region_1.0_spmd} | conditional | flops 3825205248 | bytes 24000120 | solution.py:1423
  13.1 19.3 %encoder_forward.3 = (bf16[256,768]{1,0:T(8,128)(2,1)}, bf16[256,768]{1,0:T(8,128)(2,1)}, bf16[256,768]{1,0:T(8,128)(2,1)}, bf16[256,768]{1,0:T(8,128)(2,1)}, bf...) custom-call(bf16[2,512,768]{2,1,0:T(8,128)(2,1)} %get-tuple-element., ...), custom_call_target="tpu_custom_call" | custom-call | flops 3825205248 | bytes 24000000 | tf_op jit(solution)/shard_map/cond/branch_1_fun/encoder_forward/pallas_call | solution.py:472
  32.4 2.1 collective-permute-start.5
  34.5 18.8 %conditional.7 = (bf16[256,768]{1,0:T(8,128)(2,1)}, bf16[256,768]{1,0:T(8,128)(2,1)}, bf16[256,768]{1,0:T(8,128)(2,1)}, bf16[256,768]{1,0:T(8,128)(2,1)}, bf16[2...) conditional(s32[]{:T(128)} %convert_element_type.33, () %tuple.67, ...), branch_computations={%region_2.0_spmd.clone, %region_3.0_spmd.clone} | conditional | flops 3825205248 | bytes 26359444 | solution.py:1423
  34.5 18.0 %encoder_forward.4 = (bf16[256,768]{1,0:T(8,128)(2,1)S(1)}, bf16[256,768]{1,0:T(8,128)(2,1)}, bf16[256,768]{1,0:T(8,128)(2,1)}, bf16[256,768]{1,0:T(8,128)(2,1)}...) custom-call(bf16[2,512,768]{2,1,0:T(8,128)(2,1)} %get-tuple-element., ...), custom_call_target="tpu_custom_call" | custom-call | flops 3825205248 | bytes 24000000 | tf_op jit(solution)/shard_map/cond/branch_1_fun/encoder_forward/pallas_call | solution.py:472
  52.5 0.0 copy-start.7
  52.5 0.7 copy-done.7
  53.2 2.0 collective-permute-start.6
  55.3 30.8 %conditional.8 = (bf16[256,768]{1,0:T(8,128)(2,1)}, bf16[256,768]{1,0:T(8,128)(2,1)}, f32[512,768]{1,0:T(8,128)}, f32[8,768]{1,0:T(8,128)}, f32[2,1,1536]{2,1,0:...) conditional(s32[]{:T(128)} %convert_element_type.33, ...), branch_computations={%region_4.0_spmd, %region_5.0_spmd} | conditional | flops 9261023232 | bytes 24000128 | solution.py:1458
  55.5 30.6 %encoder_targets.1 = bf16[2,256,768]{2,1,0:T(8,128)(2,1)} custom-call(bf16[2,512,768]{2,1,0:T(8,128)(2,1)} %get-tuple-element.447.patch_ref, s32[2,512,1]{2,1,0:T(8,128)S(1)} %get-tuple-element.448.order_ref, f32[8,768]{1,0:T(8,128)S(1)} %get-tuple-element.449.vec_ref, f32[2,1,1536]{2,1,0:T(1,128)S(1)} %get-tuple-element.450.bias_ref, ...), custom_call_target="tpu_custom_call" | custom-call | flops 3825205248 | bytes 24000000 | tf_op jit(solution)/shard_map/cond/branch_1_fun/encoder_targets/pallas_call | solution.py:472
  86.1 1.3 collective-permute-start.7
  87.5 0.2 conditional.9
  87.7 0.0 copy-start.3
  87.7 1.4 collective-permute-start.8
  89.2 0.0 copy-start.2
  89.2 2.3 maximum_select_fusion
  91.5 2.1 fusion
  93.7 6.1 %collective-permute-done.7 = bf16[256,768]{1,0:T(8,128)(2,1)} collective-permute-done((bf16[256,768]{1,0:T(8,128)(2,1)}, bf16[256,768]{1,0:T(8,128)(2,1)}, u32[]{:S(2)}, u32[]{:S(2)}) %collective-permute-start.7) | collective-permute-done | bytes 393248 | tf_op jit(solution)/shard_map/ppermute | solution.py:1463
  99.7 23.9 %conditional.10 = ((f32[512,768]{1,0:T(8,128)}, f32[8,768]{1,0:T(8,128)}, f32[2,1,1536]{2,1,0:T(1,128)S(1)}, bf16[256,768]{1,0:T(8,128)(2,1)}, bf16[2,256,1536]{...) conditional(s32[]{:T(128)} %convert_element_type.33, ...), branch_computations={%region_8.0_spmd, %region_9.0_spmd} | conditional | flops 3825205248 | bytes 24004104 | solution.py:1482
  99.7 0.6 slice.18.order_ref
  100.3 23.3 %encoder_backward.2 = (f32[512,768]{1,0:T(8,128)}, f32[8,768]{1,0:T(8,128)}, f32[2,1,1536]{2,1,0:T(1,128)S(1)}, bf16[256,768]{1,0:T(8,128)(2,1)}, bf16[2,256,153...) custom-call(bf16[256,768]{1,0:T(8,128)(2,1)} %get-tuple-element.482., ...), custom_call_target="tpu_custom_call" | custom-call | flops 3825205248 | bytes 24000000 | tf_op jit(solution)/shard_map/cond/branch_1_fun/encoder_backward/pallas_call | solution.py:555
  123.6 17.2 %collective-permute-done.8 = bf16[256,768]{1,0:T(8,128)(2,1)} collective-permute-done((bf16[256,768]{1,0:T(8,128)(2,1)}, bf16[256,768]{1,0:T(8,128)(2,1)}, u32[]{:S(2)}, u32[]{:S(2)}) %collective-permute-start.8) | collective-permute-done | bytes 393248 | tf_op jit(solution)/shard_map/ppermute | solution.py:1463
  140.9 23.9 %conditional.11 = ((f32[512,768]{1,0:T(8,128)}, f32[8,768]{1,0:T(8,128)}, f32[2,1,1536]{2,1,0:T(1,128)}, bf16[256,768]{1,0:T(8,128)(2,1)}, bf16[2,256,1536]{2,1,...) conditional(s32[]{:T(128)} %convert_element_type.33, ...), branch_computations={%region_10.0_spmd, %region_11.0_spmd} | conditional | flops 3825205248 | bytes 24004104 | solution.py:1482
  140.9 0.6 slice.19.order_ref
  141.5 23.3 %encoder_backward.3 = (f32[512,768]{1,0:T(8,128)}, f32[8,768]{1,0:T(8,128)}, f32[2,1,1536]{2,1,0:T(1,128)}, bf16[256,768]{1,0:T(8,128)(2,1)}, bf16[2,256,1536]{2...) custom-call(bf16[256,768]{1,0:T(8,128)(2,1)} %get-tuple-element.512., ...), custom_call_target="tpu_custom_call" | custom-call | flops 3825205248 | bytes 24000000 | tf_op jit(solution)/shard_map/cond/branch_1_fun/encoder_backward/pallas_call | solution.py:555
  164.8 157.3 %gradient_exchange.1 = (bf16[1,1536,768]{2,1,0:T(8,128)(2,1)}, bf16[1,768,1536]{2,1,0:T(8,128)(2,1)}, bf16[1,384,768]{2,1,0:T(8,128)(2,1)}, bf16[1,3,768,384]{3,...) custom-call(bf16[256,768]{1,0:T(8,128)(2,1)} %get-tuple-element.664.refs_0_, ...), custom_call_target="tpu_custom_call" | custom-call | bytes 200000000 | tf_op jit(solution)/shard_map/gradient_exchange/pallas_call | solution.py:1312
  322.1 1.5 slice_bitcast_fusion
  323.7 2.0 fusion.1
  325.7 0.6 copy.29
  326.3 2.2 convert_element_type.36
  328.4 2.0 convert_element_type.35
  330.4 0.8 copy-done.5
  331.2 2.8 convert_element_type.37
  334.1 2.6 convert_element_type.38
  336.7 0.7 copy-done.11
  337.4 1.9 maximum_bitcast_fusion
  (38 shorter events, 0.1 us)
Async XLA Ops:
  0.6 12.4 %collective-permute-start.3 = (bf16[768,1536]{1,0:T(8,128)(2,1)}, bf16[768,1536]{1,0:T(8,128)(2,1)S(1)}, u32[]{:S(2)}, u32[]{:S(2)}) collective-permute-start(bf16[768,1536]{1,0:T(8,128)(2,1)} %bitcast.33), channel_id=1, source_target_pairs={{0,1},{1,0},{2,3},{3,2},{4,5},{5,4},{6,7},{7,6},{8,9},{9,8},{10,11... | collective-permute-start | bytes 7077896 | tf_op jit(solution)/shard_map/ppermute | solution.py:1382
  1.2 11.9 %collective-permute-start.4 = (bf16[1536,768]{1,0:T(8,128)(2,1)}, bf16[1536,768]{1,0:T(8,128)(2,1)}, u32[]{:S(2)}, u32[]{:S(2)}) collective-permute-start(bf16[1536,768]{1,0:T(8,128)(2,1)} %bitcast.41), channel_id=1, source_target_pairs={{0,1},{1,0},{2,3},{3,2},{4,5},{5,4},{6,7},{7,6},{8,9},{9,8},{10,11... | collective-permute-start | bytes 7077896 | tf_op jit(solution)/shard_map/ppermute | solution.py:1382
  1.3 11.8 %collective-permute-start.1 = (bf16[3,768,384]{2,1,0:T(8,128)(2,1)}, bf16[3,768,384]{2,1,0:T(8,128)(2,1)}, u32[]{:S(2)}, u32[]{:S(2)}) collective-permute-start(bf16[3,768,384]{2,1,0:T(8,128)(2,1)} %bitcast.49), channel_id=1, source_target_pairs={{0,1},{1,0},{2,3},{3,2},{4,5},{5,4},{6,7},{7,6},{8,9},{9,8},{10,11... | collective-permute-start | bytes 5308424 | tf_op jit(solution)/shard_map/ppermute | solution.py:1382
  1.7 11.3 %collective-permute-start.2 = (bf16[384,768]{1,0:T(8,128)(2,1)}, bf16[384,768]{1,0:T(8,128)(2,1)S(1)}, u32[]{:S(2)}, u32[]{:S(2)}) collective-permute-start(bf16[384,768]{1,0:T(8,128)(2,1)} %bitcast.57), channel_id=1, source_target_pairs={{0,1},{1,0},{2,3},{3,2},{4,5},{5,4},{6,7},{7,6},{8,9},{9,8},{10,11... | collective-permute-start | bytes 1769480 | tf_op jit(solution)/shard_map/ppermute | solution.py:1382
  2.5 9.8 %collective-permute-start = (bf16[1536]{0:T(1024)(128)(2,1)S(1)}, bf16[1536]{0:T(1024)(128)(2,1)S(1)}, u32[]{:S(2)}, u32[]{:S(2)}) collective-permute-start(bf16[1536]{0:T(1024)(128)(2,1)S(1)} %reduce), channel_id=1, source_target_pairs={{0,1},{1,0},{2,3},{3,2},{4,5},{5,4},{6,7},{7,6},{8,9},{9,8},{10,11... | collective-permute-start | bytes 9224 | tf_op jit(solution)/shard_map/ppermute | solution.py:1382
  4.7 82.7 %copy-start.12 = (f32[8,768]{1,0:T(8,128)}, f32[8,768]{1,0:T(8,128)S(1)}, u32[]{:S(2)}) copy-start(f32[8,768]{1,0:T(8,128)S(1)} %concatenate.13) | copy-start | bytes 73732
  13.1 74.4 %copy-start.1 = (bf16[768,1536]{1,0:T(8,128)(2,1)}, bf16[768,1536]{1,0:T(8,128)(2,1)S(1)}, u32[]{:S(2)}) copy-start(bf16[768,1536]{1,0:T(8,128)(2,1)S(1)} %collective-permute-done.3) | copy-start | bytes 7077892
  32.4 22.9 %collective-permute-start.5 = (bf16[256,768]{1,0:T(8,128)(2,1)}, bf16[256,768]{1,0:T(8,128)(2,1)}, u32[]{:S(2)}, u32[]{:S(2)}) collective-permute-start(bf16[256,768]{1,0:T(8,128)(2,1)} %get-tuple-element.630), channel_id=1, source_target_pairs={{0,16},{1,17},{2,18},{3,19},{4,20},{5,21},{6,22},{7,23},{8,24},{9,... | collective-permute-start | bytes 1179656 | tf_op jit(solution)/shard_map/ppermute | solution.py:1429
  34.5 20.8 %copy-start.14 = (s32[2,512]{1,0:T(2,128)S(1)}, s32[2,512]{1,0:T(2,128)}, u32[]{:S(2)}) copy-start(s32[2,512]{1,0:T(2,128)} %param.26) | copy-start | bytes 12292
  34.5 20.8 %copy-start.15 = (f32[768]{0:T(1024)S(1)}, f32[768]{0:T(1024)}, u32[]{:S(2)}) copy-start(f32[768]{0:T(1024)} %param.37) | copy-start | bytes 9220
  52.5 0.7 copy-start.7
  53.2 2.1 copy-start.8
  53.2 34.2 %collective-permute-start.6 = (bf16[256,768]{1,0:T(8,128)(2,1)}, bf16[256,768]{1,0:T(8,128)(2,1)}, u32[]{:S(2)}, u32[]{:S(2)}) collective-permute-start(bf16[256,768]{1,0:T(8,128)(2,1)} %get-tuple-element.631), channel_id=1, source_target_pairs={{0,16},{1,17},{2,18},{3,19},{4,20},{5,21},{6,22},{7,23},{8,24},{9,... | collective-permute-start | bytes 1179656 | tf_op jit(solution)/shard_map/ppermute | solution.py:1429
  86.1 13.6 %collective-permute-start.7 = (bf16[256,768]{1,0:T(8,128)(2,1)}, bf16[256,768]{1,0:T(8,128)(2,1)}, u32[]{:S(2)}, u32[]{:S(2)}) collective-permute-start(bf16[256,768]{1,0:T(8,128)(2,1)} %get-tuple-element.639), channel_id=1, source_target_pairs={{16,0},{17,1},{18,2},{19,3},{20,4},{21,5},{22,6},{23,7},{24,8},{25... | collective-permute-start | bytes 1179656 | tf_op jit(solution)/shard_map/ppermute | solution.py:1463
  87.5 1.7 copy-start.9
  87.7 3.8 %copy-start.3 = (bf16[2,256,768]{2,1,0:T(8,128)(2,1)S(1)}, bf16[2,256,768]{2,1,0:T(8,128)(2,1)}, u32[]{:S(2)}) copy-start(bf16[2,256,768]{2,1,0:T(8,128)(2,1)} %get-tuple-element.633) | copy-start | bytes 2359300
  87.7 3.8 %copy-start.13 = (bf16[256,768]{1,0:T(8,128)(2,1)S(1)}, bf16[256,768]{1,0:T(8,128)(2,1)}, u32[]{:S(2)}) copy-start(bf16[256,768]{1,0:T(8,128)(2,1)} %get-tuple-element.634) | copy-start | bytes 1179652
  87.7 53.1 %collective-permute-start.8 = (bf16[256,768]{1,0:T(8,128)(2,1)}, bf16[256,768]{1,0:T(8,128)(2,1)}, u32[]{:S(2)}, u32[]{:S(2)}) collective-permute-start(bf16[256,768]{1,0:T(8,128)(2,1)} %get-tuple-element.893), channel_id=1, source_target_pairs={{16,0},{17,1},{18,2},{19,3},{20,4},{21,5},{22,6},{23,7},{24,8},{25... | collective-permute-start | bytes 1179656 | tf_op jit(solution)/shard_map/ppermute | solution.py:1463
  89.2 10.5 %copy-start.2 = (bf16[1,384,768]{2,1,0:T(8,128)(2,1)S(1)}, bf16[1,384,768]{2,1,0:T(8,128)(2,1)}, u32[]{:S(2)}) copy-start(bf16[1,384,768]{2,1,0:T(8,128)(2,1)} %param.32) | copy-start | bytes 1769476
  91.5 8.2 %copy-start = (bf16[1,768,1536]{2,1,0:T(8,128)(2,1)S(1)}, bf16[1,768,1536]{2,1,0:T(8,128)(2,1)}, u32[]{:S(2)}) copy-start(bf16[1,768,1536]{2,1,0:T(8,128)(2,1)} %param.33) | copy-start | bytes 7077892
  322.1 6.3 %copy-start.6 = (bf16[1,3,768,384]{3,2,1,0:T(8,128)(2,1)S(1)}, bf16[1,3,768,384]{3,2,1,0:T(8,128)(2,1)}, u32[]{:S(2)}) copy-start(bf16[1,3,768,384]{3,2,1,0:T(8,128)(2,1)} %get-tuple-element.709) | copy-start | bytes 5308420
  328.4 2.8 copy-start.5
  331.2 2.8 copy-start.4
  334.1 2.6 copy-start.10
  334.1 3.3 copy-start.11

commit v2 on v1

--- a/solution.py
+++ b/solution.py
@@ -798,7 +798,8 @@
 
     soon = ("G", "dF", "M", "dU")
     rest = tuple(name for name in OPERANDS if name not in soon)
-    load(soon, "start")
+    load(soon[:2], "start")
+    load(soon[2:], "start")
     load(rest, "start")
 
     def unit(buffer, at):
@@ -937,6 +938,10 @@
             step = now + 1 - mine
             at, second = unit_of(step, index)
 
+            @pl.when((now == -1) & (turn == 1))
+            def _():
+                load(soon[2:], "wait")
+
             @pl.when((step >= 0) & (step < wide) & (second * step < deep))
             def _():
                 product(at, 1 - mine)
@@ -1232,7 +1237,7 @@
         return carry
 
     steps = wide - 1 + LAG * line + LAG * (line - 1) + LAG + 1
-    load(soon, "wait")
+    load(soon[:2], "wait")
     lax.fori_loop(-1, steps, step_body, 0)
 
     small_mirror_copy().wait()
@@ -1348,6 +1353,67 @@
     )(*sum(enc_operands, []), *sum(reg_operands, []), *vec_grads, *bias_grads)
 
 
+def finish_results(sums, inputs, totals, other, bias_blocks):
+    steps = 8
+    down, up, out, qkv = sums
+    rows, width = inputs[0].shape
+    hidden = down.shape[1]
+
+    def rows_spec(array, axis):
+        block = list(array.shape)
+        block[axis] //= steps
+        return pl.BlockSpec(
+            tuple(block), lambda i: tuple(i if at == axis else 0 for at in range(len(block)))
+        )
+
+    specs = [rows_spec(one, 1) for one in (down, up, out)] + [rows_spec(qkv, 2)]
+    stacked = jax.ShapeDtypeStruct((1, len(inputs), rows, width), F32)
+    small = [(1, 2, width)] * 3 + [(1, hidden), (1, width), (width,)]
+
+    def fixed(shape):
+        return pl.BlockSpec(shape, lambda i: (0,) * len(shape))
+
+    def kernel(*refs):
+        sum_refs, input_refs = refs[:4], refs[4 : 4 + len(inputs)]
+        refs = refs[4 + len(inputs) :]
+        totals_ref, other_ref, refs = refs[0], refs[1], refs[2:]
+        for source, target in zip(sum_refs, refs[:4]):
+            target[...] = source[...].astype(F32)
+        for at, source in enumerate(input_refs):
+            refs[4][0, at] = source[...]
+        gains, biases, scales, bias, down_bias, token = refs[5:]
+
+        @pl.when(pl.program_id(0) == 0)
+        def _():
+            for at, target in enumerate((gains, biases, scales)):
+                target[0] = totals_ref[2 * at : 2 * at + 2, :]
+            for at in range(bias_blocks):
+                bias[:, at * width : (at + 1) * width] = totals_ref[8 + at : 9 + at, :]
+            down_bias[...] = totals_ref[6:7, :]
+
+            @pl.when(lax.axis_index("stream") == 0)
+            def _():
+                token[...] = other_ref[7, :]
+
+            @pl.when(lax.axis_index("stream") == 1)
+            def _():
+                token[...] = totals_ref[7, :]
+
+    return pl.pallas_call(
+        kernel,
+        grid=(steps,),
+        out_shape=[jax.ShapeDtypeStruct(one.shape, F32) for one in sums]
+        + [stacked]
+        + [jax.ShapeDtypeStruct(one, F32) for one in small],
+        in_specs=specs
+        + [rows_spec(one, 0) for one in inputs]
+        + [fixed(totals.shape), fixed(other.shape)],
+        out_specs=specs + [rows_spec(stacked, 2)] + [fixed(one) for one in small],
+        compiler_params=params_of(),
+        name="finish_results",
+    )(*sums, *inputs, totals, other)
+
+
 def place_code(positions, model_width):
     half_width = model_width // 2
     frequency = jnp.exp(
@@ -1471,7 +1537,7 @@
 
         def run_backward():
             return encoder_backward(
-                image, returned[image], cotangent, order_row[:, :, :rows], kept[image], vec, matrices
+                image, returned[image], cotangent, order_row, kept[image], vec, matrices
             )
 
         def run_pass():
@@ -1491,9 +1557,11 @@
         down, up, out, qkv, totals, other = exchange(
             enc_operands, reg_operands, vec_grads, bias_grads, width, local, hidden
         )
-        down, up, out, qkv = (one.astype(F32) for one in (down, up, out, qkv))
-        bias_total = totals[8 : 8 + hidden // width].reshape(hidden)
-        token_grad = jnp.where(encoder, other[7], totals[7])
+        outs = finish_results(
+            (down, up, out, qkv), input_grads, totals, other, hidden // width
+        )
+        down, up, out, qkv, input_grad = outs[:5]
+        gains, biases, scales, bias_total, down_bias_total, token_grad = outs[5:]
     else:
         parts = lax.cond(
             encoder,
@@ -1514,21 +1582,25 @@
         bias_total = lax.psum(bias_grad[0] + swapped(bias_grad[1]), "dp")
         totals = lax.psum(vec_grad, ("dp", "head"))
         token_grad = lax.psum(jnp.where(encoder, 0.0, totals[7]), "stream")
+        bias_total = bias_total[None]
+        input_grad = jnp.stack(input_grads)[None]
+        gains, biases, scales = (totals[at : at + 2][None] for at in (0, 2, 4))
+        down_bias_total = totals[6][None]
 
     latent_out = jnp.where(encoder, jnp.stack(latents), jnp.stack(arrived))
     return (
         latent_out,
         jnp.where(encoder, targets, jnp.stack(features))[None],
-        jnp.stack(input_grads)[None],
-        totals[0:2][None],
-        totals[2:4][None],
-        totals[4:6][None],
+        input_grad,
+        gains,
+        biases,
+        scales,
         qkv,
         out,
         up,
-        bias_total[None],
+        bias_total,
         down,
-        totals[6][None],
+        down_bias_total,
         token_grad,
     )
 

time: 340 us -> 333 us (0.979)
  other arithmetic: 19.4 us -> 4.85 us
  Pallas kernels: 272 us -> 282 us
  local copies, waits for them, and re-layouts: 7.23 us -> 2.47 us
    pallas_call x0 -> x1, Pallas kernels: none -> 9.98 us  [finish_results(): pl.pallas_call(kernel, grid=(steps,), out_shape=[jax.ShapeDtypeStruct(one...]
    convert_element_type x4 -> x0, other arithmetic: 9.62 us -> none  [shards(): down, up, out, qkv = (one.astype(F32) for one in (down, up, out, qkv))]
    unnamed x32 -> x24, local copies, waits for them, and re-layouts: 3.66 us -> 0.05 us
  transfers between devices with their start and end apart: 9 -> 9, of which waited for: 3 -> 3; matrix products, arithmetic and copies ran while one was open for 2% -> 2% of each run, Pallas kernels for 21% -> 22%
where the time goes in v2:
time: 333 us; the launch traced here: 332 us
  Pallas kernels  282 us (85%)
  waiting for transfers between devices  32.5 us (10%)
  starting transfers between devices  8.45 us (3%)
  other arithmetic  4.85 us (1%)
    pallas_call x1, Pallas kernels, exchange(): pl.pallas_call(functools.partial(exchange_kernel, images), out_shape=[jax...  158 us
    pallas_call x3, Pallas kernels, encoder_forward(): pl.pallas_call(kernel, grid=(1 if save else images,), out_shape=[shape_of...  67.9 us
    pallas_call x2, Pallas kernels, encoder_backward(): pl.pallas_call(kernel, grid=(1,), out_shape=[shape_of(s) for s in out_sha...  46.7 us
    ppermute x2, waiting for transfers between devices, shards(): returned.append(lax.ppermute(outs[1], 'stream', [(1, 0)]))  24.9 us
    pallas_call x1, Pallas kernels, finish_results(): pl.pallas_call(kernel, grid=(steps,), out_shape=[jax.ShapeDtypeStruct(one...  9.98 us
    ppermute x5, waiting for transfers between devices, swapped(): return lax.ppermute(value, 'head', SWAP)  7.64 us
  transfers between devices with their start and end apart: 9, of which 3 were waited for; matrix products, arithmetic and copies ran while one was open for 2% of the time, Pallas kernels for 22%

profile of v2, /device:TPU:0, one launch (start us, length us, event | category | flops | bytes accessed | tf_op | source)
XLA Modules:
  0.0 332.4 jit_solution(5041453847195747609)
XLA Ops:
  0.6 0.6 collective-permute-start.3
  1.2 0.1 collective-permute-start.4
  1.3 0.4 collective-permute-start.1
  1.7 0.1 collective-permute-start.2
  1.8 0.7 reduce
  2.5 0.5 collective-permute-start
  3.0 0.9 copy.26
  3.9 0.8 concatenate.13
  4.7 7.6 %collective-permute-done = bf16[1536]{0:T(1024)(128)(2,1)S(1)} collective-permute-done((bf16[1536]{0:T(1024)(128)(2,1)S(1)}, bf16[1536]{0:T(1024)(128)(2,1)S(1)}, u32[]{:S(2)}, u32[]{:S(2)}) %collective-permute-start) | collective-permute-done | bytes 3104 | tf_op jit(solution)/shard_map/ppermute | solution.py:1448
  12.3 0.7 maximum_convert_fusion
  13.0 0.0 collective-permute-done.2
  13.1 0.0 collective-permute-done.1
  13.1 0.0 collective-permute-done.3
  13.1 0.0 copy-start.1
  13.1 0.0 collective-permute-done.4
  13.1 19.3 %conditional.6 = (bf16[256,768]{1,0:T(8,128)(2,1)}, bf16[256,768]{1,0:T(8,128)(2,1)}, bf16[256,768]{1,0:T(8,128)(2,1)}, bf16[256,768]{1,0:T(8,128)(2,1)}, bf16[2...) conditional(s32[]{:T(128)} %convert_element_type.21, ...), branch_computations={%region_0.0_spmd, %region_1.0_spmd} | conditional | flops 3825205248 | bytes 24000120 | solution.py:1489
  13.1 19.2 %encoder_forward.3 = (bf16[256,768]{1,0:T(8,128)(2,1)}, bf16[256,768]{1,0:T(8,128)(2,1)}, bf16[256,768]{1,0:T(8,128)(2,1)}, bf16[256,768]{1,0:T(8,128)(2,1)}, bf...) custom-call(bf16[2,512,768]{2,1,0:T(8,128)(2,1)} %get-tuple-element., ...), custom_call_target="tpu_custom_call" | custom-call | flops 3825205248 | bytes 24000000 | tf_op jit(solution)/shard_map/cond/branch_1_fun/encoder_forward/pallas_call | solution.py:472
  32.4 2.1 collective-permute-start.5
  34.5 18.8 %conditional.7 = (bf16[256,768]{1,0:T(8,128)(2,1)}, bf16[256,768]{1,0:T(8,128)(2,1)}, bf16[256,768]{1,0:T(8,128)(2,1)}, bf16[256,768]{1,0:T(8,128)(2,1)}, bf16[2...) conditional(s32[]{:T(128)} %convert_element_type.21, () %tuple.67, ...), branch_computations={%region_2.0_spmd.clone, %region_3.0_spmd.clone} | conditional | flops 3825205248 | bytes 26359444 | solution.py:1489
  34.5 18.0 %encoder_forward.4 = (bf16[256,768]{1,0:T(8,128)(2,1)S(1)}, bf16[256,768]{1,0:T(8,128)(2,1)}, bf16[256,768]{1,0:T(8,128)(2,1)}, bf16[256,768]{1,0:T(8,128)(2,1)}...) custom-call(bf16[2,512,768]{2,1,0:T(8,128)(2,1)} %get-tuple-element., ...), custom_call_target="tpu_custom_call" | custom-call | flops 3825205248 | bytes 24000000 | tf_op jit(solution)/shard_map/cond/branch_1_fun/encoder_forward/pallas_call | solution.py:472
  52.5 0.0 copy-start.6
  52.5 0.7 copy-done.6
  53.2 2.0 collective-permute-start.6
  55.3 0.0 copy-done.11
  55.3 0.0 copy-done.12
  55.3 0.0 collective-permute-done.5
  55.3 0.0 copy-done.7
  55.3 30.8 %conditional.8 = (bf16[256,768]{1,0:T(8,128)(2,1)}, bf16[256,768]{1,0:T(8,128)(2,1)}, f32[512,768]{1,0:T(8,128)}, f32[8,768]{1,0:T(8,128)}, f32[2,1,1536]{2,1,0:...) conditional(s32[]{:T(128)} %convert_element_type.21, ...), branch_computations={%region_4.0_spmd, %region_5.0_spmd} | conditional | flops 9261023232 | bytes 24000128 | solution.py:1524
  55.5 30.6 %encoder_targets.1 = bf16[2,256,768]{2,1,0:T(8,128)(2,1)} custom-call(bf16[2,512,768]{2,1,0:T(8,128)(2,1)} %get-tuple-element.447.patch_ref, s32[2,512,1]{2,1,0:T(8,128)S(1)} %get-tuple-element.448.order_ref, f32[8,768]{1,0:T(8,128)S(1)} %get-tuple-element.449.vec_ref, f32[2,1,1536]{2,1,0:T(1,128)S(1)} %get-tuple-element.450.bias_ref, ...), custom_call_target="tpu_custom_call" | custom-call | flops 3825205248 | bytes 24000000 | tf_op jit(solution)/shard_map/cond/branch_1_fun/encoder_targets/pallas_call | solution.py:472
  86.1 1.3 collective-permute-start.7
  87.4 0.0 collective-permute-done.6
  87.5 0.2 conditional.9
  87.7 0.0 copy-start.3
  87.7 1.4 collective-permute-start.8
  89.2 0.0 copy-start.2
  89.2 2.4 maximum_select_fusion
  91.6 1.0 fusion
  92.6 7.1 %collective-permute-done.7 = bf16[256,768]{1,0:T(8,128)(2,1)} collective-permute-done((bf16[256,768]{1,0:T(8,128)(2,1)}, bf16[256,768]{1,0:T(8,128)(2,1)}, u32[]{:S(2)}, u32[]{:S(2)}) %collective-permute-start.7) | collective-permute-done | bytes 393248 | tf_op jit(solution)/shard_map/ppermute | solution.py:1529
  99.7 0.0 copy-done.2
  99.7 23.3 %conditional.10 = ((f32[512,768]{1,0:T(8,128)}, f32[8,768]{1,0:T(8,128)}, f32[2,1,1536]{2,1,0:T(1,128)S(1)}, bf16[256,768]{1,0:T(8,128)(2,1)}, bf16[2,256,1536]{...) conditional(s32[]{:T(128)} %convert_element_type.21, ...), branch_computations={%region_8.0_spmd, %region_9.0_spmd} | conditional | flops 3825205248 | bytes 24000008 | solution.py:1548
  99.7 23.3 %encoder_backward.2 = (f32[512,768]{1,0:T(8,128)}, f32[8,768]{1,0:T(8,128)}, f32[2,1,1536]{2,1,0:T(1,128)S(1)}, bf16[256,768]{1,0:T(8,128)(2,1)}, bf16[2,256,153...) custom-call(bf16[256,768]{1,0:T(8,128)(2,1)} %get-tuple-element.482., ...), custom_call_target="tpu_custom_call" | custom-call | flops 3825205248 | bytes 24000000 | tf_op jit(solution)/shard_map/cond/branch_1_fun/encoder_backward/pallas_call | solution.py:555
  123.1 17.8 %collective-permute-done.8 = bf16[256,768]{1,0:T(8,128)(2,1)} collective-permute-done((bf16[256,768]{1,0:T(8,128)(2,1)}, bf16[256,768]{1,0:T(8,128)(2,1)}, u32[]{:S(2)}, u32[]{:S(2)}) %collective-permute-start.8) | collective-permute-done | bytes 393248 | tf_op jit(solution)/shard_map/ppermute | solution.py:1529
  140.8 23.3 %conditional.11 = ((f32[512,768]{1,0:T(8,128)}, f32[8,768]{1,0:T(8,128)}, f32[2,1,1536]{2,1,0:T(1,128)}, bf16[256,768]{1,0:T(8,128)(2,1)}, bf16[2,256,1536]{2,1,...) conditional(s32[]{:T(128)} %convert_element_type.21, ...), branch_computations={%region_10.0_spmd, %region_11.0_spmd} | conditional | flops 3825205248 | bytes 24000008 | solution.py:1548
  140.8 23.3 %encoder_backward.3 = (f32[512,768]{1,0:T(8,128)}, f32[8,768]{1,0:T(8,128)}, f32[2,1,1536]{2,1,0:T(1,128)}, bf16[256,768]{1,0:T(8,128)(2,1)}, bf16[2,256,1536]{2...) custom-call(bf16[256,768]{1,0:T(8,128)(2,1)} %get-tuple-element.512., ...), custom_call_target="tpu_custom_call" | custom-call | flops 3825205248 | bytes 24000000 | tf_op jit(solution)/shard_map/cond/branch_1_fun/encoder_backward/pallas_call | solution.py:555
  164.2 0.0 copy-start.4
  164.2 0.0 copy-start.5
  164.2 158.0 %gradient_exchange.1 = (bf16[1,1536,768]{2,1,0:T(8,128)(2,1)}, bf16[1,768,1536]{2,1,0:T(8,128)(2,1)}, bf16[1,384,768]{2,1,0:T(8,128)(2,1)}, bf16[1,3,768,384]{3,...) custom-call(bf16[256,768]{1,0:T(8,128)(2,1)} %get-tuple-element.660.refs_0_, ...), custom_call_target="tpu_custom_call" | custom-call | bytes 200000000 | tf_op jit(solution)/shard_map/gradient_exchange/pallas_call | solution.py:1317
  322.2 10.0 %finish_results.1 = (f32[1,1536,768]{2,1,0:T(8,128)}, f32[1,768,1536]{2,1,0:T(8,128)}, f32[1,384,768]{2,1,0:T(8,128)}, f32[1,3,768,384]{3,2,1,0:T(8,128)}, f32[1...) custom-call(bf16[1,1536,768]{2,1,0:T(8,128)(2,1)} %get-tuple-element, ...), custom_call_target="tpu_custom_call" | custom-call | tf_op jit(solution)/shard_map/finish_results/pallas_call | solution.py:1402
  (23 shorter events, 0.1 us)
Async XLA Ops:
  0.6 12.4 %collective-permute-start.3 = (bf16[768,1536]{1,0:T(8,128)(2,1)}, bf16[768,1536]{1,0:T(8,128)(2,1)S(1)}, u32[]{:S(2)}, u32[]{:S(2)}) collective-permute-start(bf16[768,1536]{1,0:T(8,128)(2,1)} %bitcast.19), channel_id=1, source_target_pairs={{0,1},{1,0},{2,3},{3,2},{4,5},{5,4},{6,7},{7,6},{8,9},{9,8},{10,11... | collective-permute-start | bytes 7077896 | tf_op jit(solution)/shard_map/ppermute | solution.py:1448
  1.2 11.9 %collective-permute-start.4 = (bf16[1536,768]{1,0:T(8,128)(2,1)}, bf16[1536,768]{1,0:T(8,128)(2,1)}, u32[]{:S(2)}, u32[]{:S(2)}) collective-permute-start(bf16[1536,768]{1,0:T(8,128)(2,1)} %bitcast.27), channel_id=1, source_target_pairs={{0,1},{1,0},{2,3},{3,2},{4,5},{5,4},{6,7},{7,6},{8,9},{9,8},{10,11... | collective-permute-start | bytes 7077896 | tf_op jit(solution)/shard_map/ppermute | solution.py:1448
  1.3 11.8 %collective-permute-start.1 = (bf16[3,768,384]{2,1,0:T(8,128)(2,1)}, bf16[3,768,384]{2,1,0:T(8,128)(2,1)}, u32[]{:S(2)}, u32[]{:S(2)}) collective-permute-start(bf16[3,768,384]{2,1,0:T(8,128)(2,1)} %bitcast.35), channel_id=1, source_target_pairs={{0,1},{1,0},{2,3},{3,2},{4,5},{5,4},{6,7},{7,6},{8,9},{9,8},{10,11... | collective-permute-start | bytes 5308424 | tf_op jit(solution)/shard_map/ppermute | solution.py:1448
  1.7 11.3 %collective-permute-start.2 = (bf16[384,768]{1,0:T(8,128)(2,1)}, bf16[384,768]{1,0:T(8,128)(2,1)S(1)}, u32[]{:S(2)}, u32[]{:S(2)}) collective-permute-start(bf16[384,768]{1,0:T(8,128)(2,1)} %bitcast.43), channel_id=1, source_target_pairs={{0,1},{1,0},{2,3},{3,2},{4,5},{5,4},{6,7},{7,6},{8,9},{9,8},{10,11... | collective-permute-start | bytes 1769480 | tf_op jit(solution)/shard_map/ppermute | solution.py:1448
  2.5 9.8 %collective-permute-start = (bf16[1536]{0:T(1024)(128)(2,1)S(1)}, bf16[1536]{0:T(1024)(128)(2,1)S(1)}, u32[]{:S(2)}, u32[]{:S(2)}) collective-permute-start(bf16[1536]{0:T(1024)(128)(2,1)S(1)} %reduce), channel_id=1, source_target_pairs={{0,1},{1,0},{2,3},{3,2},{4,5},{5,4},{6,7},{7,6},{8,9},{9,8},{10,11... | collective-permute-start | bytes 9224 | tf_op jit(solution)/shard_map/ppermute | solution.py:1448
  4.7 82.7 %copy-start.8 = (f32[8,768]{1,0:T(8,128)}, f32[8,768]{1,0:T(8,128)S(1)}, u32[]{:S(2)}) copy-start(f32[8,768]{1,0:T(8,128)S(1)} %concatenate.13) | copy-start | bytes 73732
  13.1 74.4 %copy-start.1 = (bf16[768,1536]{1,0:T(8,128)(2,1)}, bf16[768,1536]{1,0:T(8,128)(2,1)S(1)}, u32[]{:S(2)}) copy-start(bf16[768,1536]{1,0:T(8,128)(2,1)S(1)} %collective-permute-done.3) | copy-start | bytes 7077892
  32.4 22.9 %collective-permute-start.5 = (bf16[256,768]{1,0:T(8,128)(2,1)}, bf16[256,768]{1,0:T(8,128)(2,1)}, u32[]{:S(2)}, u32[]{:S(2)}) collective-permute-start(bf16[256,768]{1,0:T(8,128)(2,1)} %get-tuple-element.641), channel_id=1, source_target_pairs={{0,16},{1,17},{2,18},{3,19},{4,20},{5,21},{6,22},{7,23},{8,24},{9,... | collective-permute-start | bytes 1179656 | tf_op jit(solution)/shard_map/ppermute | solution.py:1495
  34.4 20.8 %copy-start.11 = (s32[2,512]{1,0:T(2,128)S(1)}, s32[2,512]{1,0:T(2,128)}, u32[]{:S(2)}) copy-start(s32[2,512]{1,0:T(2,128)} %param.26) | copy-start | bytes 12292
  34.4 20.8 %copy-start.12 = (f32[768]{0:T(1024)S(1)}, f32[768]{0:T(1024)}, u32[]{:S(2)}) copy-start(f32[768]{0:T(1024)} %param.37) | copy-start | bytes 9220
  52.5 0.7 copy-start.6
  53.2 2.1 copy-start.7
  53.2 34.2 %collective-permute-start.6 = (bf16[256,768]{1,0:T(8,128)(2,1)}, bf16[256,768]{1,0:T(8,128)(2,1)}, u32[]{:S(2)}, u32[]{:S(2)}) collective-permute-start(bf16[256,768]{1,0:T(8,128)(2,1)} %get-tuple-element.642), channel_id=1, source_target_pairs={{0,16},{1,17},{2,18},{3,19},{4,20},{5,21},{6,22},{7,23},{8,24},{9,... | collective-permute-start | bytes 1179656 | tf_op jit(solution)/shard_map/ppermute | solution.py:1495
  86.1 13.6 %collective-permute-start.7 = (bf16[256,768]{1,0:T(8,128)(2,1)}, bf16[256,768]{1,0:T(8,128)(2,1)}, u32[]{:S(2)}, u32[]{:S(2)}) collective-permute-start(bf16[256,768]{1,0:T(8,128)(2,1)} %get-tuple-element.650), channel_id=1, source_target_pairs={{16,0},{17,1},{18,2},{19,3},{20,4},{21,5},{22,6},{23,7},{24,8},{25... | collective-permute-start | bytes 1179656 | tf_op jit(solution)/shard_map/ppermute | solution.py:1529
  87.7 3.9 %copy-start.3 = (bf16[2,256,768]{2,1,0:T(8,128)(2,1)S(1)}, bf16[2,256,768]{2,1,0:T(8,128)(2,1)}, u32[]{:S(2)}) copy-start(bf16[2,256,768]{2,1,0:T(8,128)(2,1)} %get-tuple-element.644) | copy-start | bytes 2359300
  87.7 3.9 %copy-start.9 = (bf16[256,768]{1,0:T(8,128)(2,1)S(1)}, bf16[256,768]{1,0:T(8,128)(2,1)}, u32[]{:S(2)}) copy-start(bf16[256,768]{1,0:T(8,128)(2,1)} %get-tuple-element.645) | copy-start | bytes 1179652
  87.7 3.9 %copy-start.10 = (bf16[256,768]{1,0:T(8,128)(2,1)S(1)}, bf16[256,768]{1,0:T(8,128)(2,1)}, u32[]{:S(2)}) copy-start(bf16[256,768]{1,0:T(8,128)(2,1)} %get-tuple-element.901) | copy-start | bytes 1179652
  87.7 53.1 %collective-permute-start.8 = (bf16[256,768]{1,0:T(8,128)(2,1)}, bf16[256,768]{1,0:T(8,128)(2,1)}, u32[]{:S(2)}, u32[]{:S(2)}) collective-permute-start(bf16[256,768]{1,0:T(8,128)(2,1)} %get-tuple-element.915), channel_id=1, source_target_pairs={{16,0},{17,1},{18,2},{19,3},{20,4},{21,5},{22,6},{23,7},{24,8},{25... | collective-permute-start | bytes 1179656 | tf_op jit(solution)/shard_map/ppermute | solution.py:1529
  89.2 10.6 %copy-start.2 = (bf16[1,384,768]{2,1,0:T(8,128)(2,1)S(1)}, bf16[1,384,768]{2,1,0:T(8,128)(2,1)}, u32[]{:S(2)}) copy-start(bf16[1,384,768]{2,1,0:T(8,128)(2,1)} %param.32) | copy-start | bytes 1769476
  91.6 8.1 %copy-start = (bf16[1,768,1536]{2,1,0:T(8,128)(2,1)S(1)}, bf16[1,768,1536]{2,1,0:T(8,128)(2,1)}, u32[]{:S(2)}) copy-start(bf16[1,768,1536]{2,1,0:T(8,128)(2,1)} %param.33) | copy-start | bytes 7077892
  164.2 158.0 %copy-start.4 = (f32[512,768]{1,0:T(8,128)S(1)}, f32[512,768]{1,0:T(8,128)}, u32[]{:S(2)}) copy-start(f32[512,768]{1,0:T(8,128)} %get-tuple-element.721.refs_4_) | copy-start | bytes 4718596
  164.2 158.0 %copy-start.5 = (f32[512,768]{1,0:T(8,128)S(1)}, f32[512,768]{1,0:T(8,128)}, u32[]{:S(2)}) copy-start(f32[512,768]{1,0:T(8,128)} %get-tuple-element.722.refs_5_) | copy-start | bytes 4718596

commit v3 on v2

--- a/solution.py
+++ b/solution.py
@@ -195,7 +195,7 @@
     weights.wait("down")
     fed = keep["F"]
     fed[...] = jnp.broadcast_to(vec[6:7, :], fed.shape)
-    step = 512
+    step = 768
     per_half = weights["up"].shape[2] // step
 
     def feed(index, carry):
@@ -245,7 +245,7 @@
     weights.wait("up")
     grad_mid = work["dM"]
     grad_mid[...] = jnp.zeros_like(grad_mid)
-    step = 512
+    step = 768
     per_half = weights["up"].shape[2] // step
 
     def feed(index, carry):

time: 333 us -> 329 us (0.988)
  transfers between devices with their start and end apart: 9 -> 9, of which waited for: 3 -> 3; matrix products, arithmetic and copies ran while one was open for 2% -> 2% of each run, Pallas kernels for 22% -> 21%
where the time goes in v3:
time: 329 us; the launch traced here: 328 us
  Pallas kernels  279 us (85%)
  waiting for transfers between devices  32.1 us (10%)
  starting transfers between devices  8.45 us (3%)
  other arithmetic  4.85 us (1%)
    pallas_call x1, Pallas kernels, exchange(): pl.pallas_call(functools.partial(exchange_kernel, images), out_shape=[jax...  158 us
    pallas_call x3, Pallas kernels, encoder_forward(): pl.pallas_call(kernel, grid=(1 if save else images,), out_shape=[shape_of...  65.6 us
    pallas_call x2, Pallas kernels, encoder_backward(): pl.pallas_call(kernel, grid=(1,), out_shape=[shape_of(s) for s in out_sha...  45.4 us
    ppermute x2, waiting for transfers between devices, shards(): returned.append(lax.ppermute(outs[1], 'stream', [(1, 0)]))  24.4 us
    pallas_call x1, Pallas kernels, finish_results(): pl.pallas_call(kernel, grid=(steps,), out_shape=[jax.ShapeDtypeStruct(one...  9.98 us
    ppermute x5, waiting for transfers between devices, swapped(): return lax.ppermute(value, 'head', SWAP)  7.64 us
  transfers between devices with their start and end apart: 9, of which 3 were waited for; matrix products, arithmetic and copies ran while one was open for 2% of the time, Pallas kernels for 21%

profile of v3, /device:TPU:0, one launch (start us, length us, event | category | flops | bytes accessed | tf_op | source)
XLA Modules:
  0.0 328.4 jit_solution(15039184204998842056)
XLA Ops:
  0.6 0.6 collective-permute-start.3
  1.2 0.1 collective-permute-start.4
  1.3 0.4 collective-permute-start.1
  1.7 0.1 collective-permute-start.2
  1.8 0.7 reduce
  2.5 0.5 collective-permute-start
  3.0 0.9 copy.26
  3.9 0.8 concatenate.13
  4.7 7.6 %collective-permute-done = bf16[1536]{0:T(1024)(128)(2,1)S(1)} collective-permute-done((bf16[1536]{0:T(1024)(128)(2,1)S(1)}, bf16[1536]{0:T(1024)(128)(2,1)S(1)}, u32[]{:S(2)}, u32[]{:S(2)}) %collective-permute-start) | collective-permute-done | bytes 3104 | tf_op jit(solution)/shard_map/ppermute | solution.py:1448
  12.3 0.7 maximum_convert_fusion
  13.0 0.0 collective-permute-done.2
  13.1 0.0 collective-permute-done.1
  13.1 0.0 collective-permute-done.3
  13.1 0.0 copy-start.1
  13.1 0.0 collective-permute-done.4
  13.1 18.8 %conditional.6 = (bf16[256,768]{1,0:T(8,128)(2,1)}, bf16[256,768]{1,0:T(8,128)(2,1)}, bf16[256,768]{1,0:T(8,128)(2,1)}, bf16[256,768]{1,0:T(8,128)(2,1)}, bf16[2...) conditional(s32[]{:T(128)} %convert_element_type.21, ...), branch_computations={%region_0.0_spmd, %region_1.0_spmd} | conditional | flops 3825205248 | bytes 24000120 | solution.py:1489
  13.1 18.8 %encoder_forward.3 = (bf16[256,768]{1,0:T(8,128)(2,1)}, bf16[256,768]{1,0:T(8,128)(2,1)}, bf16[256,768]{1,0:T(8,128)(2,1)}, bf16[256,768]{1,0:T(8,128)(2,1)}, bf...) custom-call(bf16[2,512,768]{2,1,0:T(8,128)(2,1)} %get-tuple-element., ...), custom_call_target="tpu_custom_call" | custom-call | flops 3825205248 | bytes 24000000 | tf_op jit(solution)/shard_map/cond/branch_1_fun/encoder_forward/pallas_call | solution.py:472
  31.9 2.1 collective-permute-start.5
  34.0 18.3 %conditional.7 = (bf16[256,768]{1,0:T(8,128)(2,1)}, bf16[256,768]{1,0:T(8,128)(2,1)}, bf16[256,768]{1,0:T(8,128)(2,1)}, bf16[256,768]{1,0:T(8,128)(2,1)}, bf16[2...) conditional(s32[]{:T(128)} %convert_element_type.21, () %tuple.67, ...), branch_computations={%region_2.0_spmd.clone, %region_3.0_spmd.clone} | conditional | flops 3825205248 | bytes 26359444 | solution.py:1489
  34.0 17.5 %encoder_forward.4 = (bf16[256,768]{1,0:T(8,128)(2,1)S(1)}, bf16[256,768]{1,0:T(8,128)(2,1)}, bf16[256,768]{1,0:T(8,128)(2,1)}, bf16[256,768]{1,0:T(8,128)(2,1)}...) custom-call(bf16[2,512,768]{2,1,0:T(8,128)(2,1)} %get-tuple-element., ...), custom_call_target="tpu_custom_call" | custom-call | flops 3825205248 | bytes 24000000 | tf_op jit(solution)/shard_map/cond/branch_1_fun/encoder_forward/pallas_call | solution.py:472
  51.5 0.0 copy-start.6
  51.5 0.7 copy-done.6
  52.2 2.0 collective-permute-start.6
  54.3 0.0 copy-done.11
  54.3 0.0 collective-permute-done.5
  54.3 0.0 copy-done.7
  54.3 29.6 %conditional.8 = (bf16[256,768]{1,0:T(8,128)(2,1)}, bf16[256,768]{1,0:T(8,128)(2,1)}, f32[512,768]{1,0:T(8,128)}, f32[8,768]{1,0:T(8,128)}, f32[2,1,1536]{2,1,0:...) conditional(s32[]{:T(128)} %convert_element_type.21, ...), branch_computations={%region_4.0_spmd, %region_5.0_spmd} | conditional | flops 9261023232 | bytes 24000128 | solution.py:1524
  54.5 29.3 %encoder_targets.1 = bf16[2,256,768]{2,1,0:T(8,128)(2,1)} custom-call(bf16[2,512,768]{2,1,0:T(8,128)(2,1)} %get-tuple-element.447.patch_ref, s32[2,512,1]{2,1,0:T(8,128)S(1)} %get-tuple-element.448.order_ref, f32[8,768]{1,0:T(8,128)S(1)} %get-tuple-element.449.vec_ref, f32[2,1,1536]{2,1,0:T(1,128)S(1)} %get-tuple-element.450.bias_ref, ...), custom_call_target="tpu_custom_call" | custom-call | flops 3825205248 | bytes 24000000 | tf_op jit(solution)/shard_map/cond/branch_1_fun/encoder_targets/pallas_call | solution.py:472
  83.9 1.3 collective-permute-start.7
  85.2 0.0 collective-permute-done.6
  85.2 0.0 copy-done.8
  85.2 0.0 copy-done.1
  85.2 0.2 conditional.9
  85.5 0.0 copy-start.3
  85.5 0.0 copy-start.9
  85.5 0.0 copy-start.10
  85.5 1.4 collective-permute-start.8
  86.9 0.0 copy-start.2
  87.0 2.4 maximum_select_fusion
  89.4 1.0 fusion
  90.4 7.1 %collective-permute-done.7 = bf16[256,768]{1,0:T(8,128)(2,1)} collective-permute-done((bf16[256,768]{1,0:T(8,128)(2,1)}, bf16[256,768]{1,0:T(8,128)(2,1)}, u32[]{:S(2)}, u32[]{:S(2)}) %collective-permute-start.7) | collective-permute-done | bytes 393248 | tf_op jit(solution)/shard_map/ppermute | solution.py:1529
  97.5 22.7 %conditional.10 = ((f32[512,768]{1,0:T(8,128)}, f32[8,768]{1,0:T(8,128)}, f32[2,1,1536]{2,1,0:T(1,128)S(1)}, bf16[256,768]{1,0:T(8,128)(2,1)}, bf16[2,256,1536]{...) conditional(s32[]{:T(128)} %convert_element_type.21, ...), branch_computations={%region_8.0_spmd, %region_9.0_spmd} | conditional | flops 3825205248 | bytes 24000008 | solution.py:1548
  97.5 22.7 %encoder_backward.2 = (f32[512,768]{1,0:T(8,128)}, f32[8,768]{1,0:T(8,128)}, f32[2,1,1536]{2,1,0:T(1,128)S(1)}, bf16[256,768]{1,0:T(8,128)(2,1)}, bf16[2,256,153...) custom-call(bf16[256,768]{1,0:T(8,128)(2,1)} %get-tuple-element.482., ...), custom_call_target="tpu_custom_call" | custom-call | flops 3825205248 | bytes 24000000 | tf_op jit(solution)/shard_map/cond/branch_1_fun/encoder_backward/pallas_call | solution.py:555
  120.2 17.3 %collective-permute-done.8 = bf16[256,768]{1,0:T(8,128)(2,1)} collective-permute-done((bf16[256,768]{1,0:T(8,128)(2,1)}, bf16[256,768]{1,0:T(8,128)(2,1)}, u32[]{:S(2)}, u32[]{:S(2)}) %collective-permute-start.8) | collective-permute-done | bytes 393248 | tf_op jit(solution)/shard_map/ppermute | solution.py:1529
  137.5 22.7 %conditional.11 = ((f32[512,768]{1,0:T(8,128)}, f32[8,768]{1,0:T(8,128)}, f32[2,1,1536]{2,1,0:T(1,128)}, bf16[256,768]{1,0:T(8,128)(2,1)}, bf16[2,256,1536]{2,1,...) conditional(s32[]{:T(128)} %convert_element_type.21, ...), branch_computations={%region_10.0_spmd, %region_11.0_spmd} | conditional | flops 3825205248 | bytes 24000008 | solution.py:1548
  137.5 22.7 %encoder_backward.3 = (f32[512,768]{1,0:T(8,128)}, f32[8,768]{1,0:T(8,128)}, f32[2,1,1536]{2,1,0:T(1,128)}, bf16[256,768]{1,0:T(8,128)(2,1)}, bf16[2,256,1536]{2...) custom-call(bf16[256,768]{1,0:T(8,128)(2,1)} %get-tuple-element.512., ...), custom_call_target="tpu_custom_call" | custom-call | flops 3825205248 | bytes 24000000 | tf_op jit(solution)/shard_map/cond/branch_1_fun/encoder_backward/pallas_call | solution.py:555
  160.2 158.0 %gradient_exchange.1 = (bf16[1,1536,768]{2,1,0:T(8,128)(2,1)}, bf16[1,768,1536]{2,1,0:T(8,128)(2,1)}, bf16[1,384,768]{2,1,0:T(8,128)(2,1)}, bf16[1,3,768,384]{3,...) custom-call(bf16[256,768]{1,0:T(8,128)(2,1)} %get-tuple-element.660.refs_0_, ...), custom_call_target="tpu_custom_call" | custom-call | bytes 200000000 | tf_op jit(solution)/shard_map/gradient_exchange/pallas_call | solution.py:1317
  318.2 10.0 %finish_results.1 = (f32[1,1536,768]{2,1,0:T(8,128)}, f32[1,768,1536]{2,1,0:T(8,128)}, f32[1,384,768]{2,1,0:T(8,128)}, f32[1,3,768,384]{3,2,1,0:T(8,128)}, f32[1...) custom-call(bf16[1,1536,768]{2,1,0:T(8,128)(2,1)} %get-tuple-element, ...), custom_call_target="tpu_custom_call" | custom-call | tf_op jit(solution)/shard_map/finish_results/pallas_call | solution.py:1402
  (23 shorter events, 0.1 us)
Async XLA Ops:
  0.6 12.4 %collective-permute-start.3 = (bf16[768,1536]{1,0:T(8,128)(2,1)}, bf16[768,1536]{1,0:T(8,128)(2,1)S(1)}, u32[]{:S(2)}, u32[]{:S(2)}) collective-permute-start(bf16[768,1536]{1,0:T(8,128)(2,1)} %bitcast.19), channel_id=1, source_target_pairs={{0,1},{1,0},{2,3},{3,2},{4,5},{5,4},{6,7},{7,6},{8,9},{9,8},{10,11... | collective-permute-start | bytes 7077896 | tf_op jit(solution)/shard_map/ppermute | solution.py:1448
  1.2 11.9 %collective-permute-start.4 = (bf16[1536,768]{1,0:T(8,128)(2,1)}, bf16[1536,768]{1,0:T(8,128)(2,1)}, u32[]{:S(2)}, u32[]{:S(2)}) collective-permute-start(bf16[1536,768]{1,0:T(8,128)(2,1)} %bitcast.27), channel_id=1, source_target_pairs={{0,1},{1,0},{2,3},{3,2},{4,5},{5,4},{6,7},{7,6},{8,9},{9,8},{10,11... | collective-permute-start | bytes 7077896 | tf_op jit(solution)/shard_map/ppermute | solution.py:1448
  1.3 11.8 %collective-permute-start.1 = (bf16[3,768,384]{2,1,0:T(8,128)(2,1)}, bf16[3,768,384]{2,1,0:T(8,128)(2,1)}, u32[]{:S(2)}, u32[]{:S(2)}) collective-permute-start(bf16[3,768,384]{2,1,0:T(8,128)(2,1)} %bitcast.35), channel_id=1, source_target_pairs={{0,1},{1,0},{2,3},{3,2},{4,5},{5,4},{6,7},{7,6},{8,9},{9,8},{10,11... | collective-permute-start | bytes 5308424 | tf_op jit(solution)/shard_map/ppermute | solution.py:1448
  1.7 11.3 %collective-permute-start.2 = (bf16[384,768]{1,0:T(8,128)(2,1)}, bf16[384,768]{1,0:T(8,128)(2,1)S(1)}, u32[]{:S(2)}, u32[]{:S(2)}) collective-permute-start(bf16[384,768]{1,0:T(8,128)(2,1)} %bitcast.43), channel_id=1, source_target_pairs={{0,1},{1,0},{2,3},{3,2},{4,5},{5,4},{6,7},{7,6},{8,9},{9,8},{10,11... | collective-permute-start | bytes 1769480 | tf_op jit(solution)/shard_map/ppermute | solution.py:1448
  2.5 9.8 %collective-permute-start = (bf16[1536]{0:T(1024)(128)(2,1)S(1)}, bf16[1536]{0:T(1024)(128)(2,1)S(1)}, u32[]{:S(2)}, u32[]{:S(2)}) collective-permute-start(bf16[1536]{0:T(1024)(128)(2,1)S(1)} %reduce), channel_id=1, source_target_pairs={{0,1},{1,0},{2,3},{3,2},{4,5},{5,4},{6,7},{7,6},{8,9},{9,8},{10,11... | collective-permute-start | bytes 9224 | tf_op jit(solution)/shard_map/ppermute | solution.py:1448
  4.7 80.5 %copy-start.8 = (f32[8,768]{1,0:T(8,128)}, f32[8,768]{1,0:T(8,128)S(1)}, u32[]{:S(2)}) copy-start(f32[8,768]{1,0:T(8,128)S(1)} %concatenate.13) | copy-start | bytes 73732
  13.1 72.1 %copy-start.1 = (bf16[768,1536]{1,0:T(8,128)(2,1)}, bf16[768,1536]{1,0:T(8,128)(2,1)S(1)}, u32[]{:S(2)}) copy-start(bf16[768,1536]{1,0:T(8,128)(2,1)S(1)} %collective-permute-done.3) | copy-start | bytes 7077892
  31.9 22.4 %collective-permute-start.5 = (bf16[256,768]{1,0:T(8,128)(2,1)}, bf16[256,768]{1,0:T(8,128)(2,1)}, u32[]{:S(2)}, u32[]{:S(2)}) collective-permute-start(bf16[256,768]{1,0:T(8,128)(2,1)} %get-tuple-element.641), channel_id=1, source_target_pairs={{0,16},{1,17},{2,18},{3,19},{4,20},{5,21},{6,22},{7,23},{8,24},{9,... | collective-permute-start | bytes 1179656 | tf_op jit(solution)/shard_map/ppermute | solution.py:1495
  34.0 20.3 %copy-start.11 = (s32[2,512]{1,0:T(2,128)S(1)}, s32[2,512]{1,0:T(2,128)}, u32[]{:S(2)}) copy-start(s32[2,512]{1,0:T(2,128)} %param.26) | copy-start | bytes 12292
  34.0 20.3 %copy-start.12 = (f32[768]{0:T(1024)S(1)}, f32[768]{0:T(1024)}, u32[]{:S(2)}) copy-start(f32[768]{0:T(1024)} %param.37) | copy-start | bytes 9220
  51.5 0.7 copy-start.6
  52.2 2.1 copy-start.7
  52.2 32.9 %collective-permute-start.6 = (bf16[256,768]{1,0:T(8,128)(2,1)}, bf16[256,768]{1,0:T(8,128)(2,1)}, u32[]{:S(2)}, u32[]{:S(2)}) collective-permute-start(bf16[256,768]{1,0:T(8,128)(2,1)} %get-tuple-element.642), channel_id=1, source_target_pairs={{0,16},{1,17},{2,18},{3,19},{4,20},{5,21},{6,22},{7,23},{8,24},{9,... | collective-permute-start | bytes 1179656 | tf_op jit(solution)/shard_map/ppermute | solution.py:1495
  83.9 13.6 %collective-permute-start.7 = (bf16[256,768]{1,0:T(8,128)(2,1)}, bf16[256,768]{1,0:T(8,128)(2,1)}, u32[]{:S(2)}, u32[]{:S(2)}) collective-permute-start(bf16[256,768]{1,0:T(8,128)(2,1)} %get-tuple-element.650), channel_id=1, source_target_pairs={{16,0},{17,1},{18,2},{19,3},{20,4},{21,5},{22,6},{23,7},{24,8},{25... | collective-permute-start | bytes 1179656 | tf_op jit(solution)/shard_map/ppermute | solution.py:1529
  85.5 3.9 %copy-start.3 = (bf16[2,256,768]{2,1,0:T(8,128)(2,1)S(1)}, bf16[2,256,768]{2,1,0:T(8,128)(2,1)}, u32[]{:S(2)}) copy-start(bf16[2,256,768]{2,1,0:T(8,128)(2,1)} %get-tuple-element.644) | copy-start | bytes 2359300
  85.5 3.9 %copy-start.9 = (bf16[256,768]{1,0:T(8,128)(2,1)S(1)}, bf16[256,768]{1,0:T(8,128)(2,1)}, u32[]{:S(2)}) copy-start(bf16[256,768]{1,0:T(8,128)(2,1)} %get-tuple-element.645) | copy-start | bytes 1179652
  85.5 3.9 %copy-start.10 = (bf16[256,768]{1,0:T(8,128)(2,1)S(1)}, bf16[256,768]{1,0:T(8,128)(2,1)}, u32[]{:S(2)}) copy-start(bf16[256,768]{1,0:T(8,128)(2,1)} %get-tuple-element.901) | copy-start | bytes 1179652
  85.5 52.0 %collective-permute-start.8 = (bf16[256,768]{1,0:T(8,128)(2,1)}, bf16[256,768]{1,0:T(8,128)(2,1)}, u32[]{:S(2)}, u32[]{:S(2)}) collective-permute-start(bf16[256,768]{1,0:T(8,128)(2,1)} %get-tuple-element.915), channel_id=1, source_target_pairs={{16,0},{17,1},{18,2},{19,3},{20,4},{21,5},{22,6},{23,7},{24,8},{25... | collective-permute-start | bytes 1179656 | tf_op jit(solution)/shard_map/ppermute | solution.py:1529
  86.9 10.6 %copy-start.2 = (bf16[1,384,768]{2,1,0:T(8,128)(2,1)S(1)}, bf16[1,384,768]{2,1,0:T(8,128)(2,1)}, u32[]{:S(2)}) copy-start(bf16[1,384,768]{2,1,0:T(8,128)(2,1)} %param.32) | copy-start | bytes 1769476
  89.4 8.1 %copy-start = (bf16[1,768,1536]{2,1,0:T(8,128)(2,1)S(1)}, bf16[1,768,1536]{2,1,0:T(8,128)(2,1)}, u32[]{:S(2)}) copy-start(bf16[1,768,1536]{2,1,0:T(8,128)(2,1)} %param.33) | copy-start | bytes 7077892
  160.2 158.0 %copy-start.4 = (f32[512,768]{1,0:T(8,128)S(1)}, f32[512,768]{1,0:T(8,128)}, u32[]{:S(2)}) copy-start(f32[512,768]{1,0:T(8,128)} %get-tuple-element.721.refs_4_) | copy-start | bytes 4718596
  160.2 158.0 %copy-start.5 = (f32[512,768]{1,0:T(8,128)S(1)}, f32[512,768]{1,0:T(8,128)}, u32[]{:S(2)}) copy-start(f32[512,768]{1,0:T(8,128)} %get-tuple-element.722.refs_5_) | copy-start | bytes 4718596
